TPU v7x, 512 devices: a whole 4x8x8 slice. The times are simulated.
512 devices in a mesh: srow: 32 (over y, x), scol: 16 (over z, core).
Axes of the slice: x: 4, y: 8, z: 8, core: 2. Of those that a mesh axis runs over, the one named last changes fastest.
Arguments:
- leaf_rhs: bfloat16 [32, 16, 4, 256, 512], P('srow', 'scol'), may hold values from -6 to 6
- leaf_inverse: bfloat16 [32, 16, 4, 256, 256], P('srow', 'scol'), may hold values from -0.375 to 0.375
- leaf_blocks: bfloat16 [32, 16, 4, 3, 256, 256], P('srow', 'scol'), may hold values from -0.1875 to 0.1875
- leaf_outer: bfloat16 [32, 16, 4, 256, 256], P('srow', 'scol'), may hold values from -0.046875 to 0.046875
- leaf_targets: int32 [32, 16, 4, 4], P('srow', 'scol'), may hold values 0 or 1
- level_one: bfloat16 [4096, 16, 4, 256], P('srow', 'scol'), may hold values from -0.25 to 0.25
- level_two: bfloat16 [2048, 16, 3, 256], P('srow', 'scol'), may hold values from -0.1875 to 0.1875
- level_three: bfloat16 [1024, 16, 2, 256], P('srow', 'scol'), may hold values from -0.125 to 0.125
Outputs:
- solved_one: bfloat16 [256, 16, 8192], P(None, 'scol', 'srow')
- solved_two: bfloat16 [256, 16, 4096], P(None, 'scol', 'srow')
- solved_three: bfloat16 [256, 16, 2048], P(None, 'scol', 'srow')
- outer_update: float32 [256, 2048], P('scol', 'srow')
Inputs may be any that keep to these rules, and one draw needn't show every extreme that they name: `leaf_targets`: 1 marks a block that is present in the leaf's panel, 0 one that is absent.
All inputs are finite; a program needn't handle non-finite values.
Results may differ from a plain program's by a relative error of at most 0.0049.
Values may be sent and summed in bfloat16 or wider, within the bound.
No kernel may reach another device: no remote copies, remote signals or barrier semaphores. Data moves between devices by JAX's collectives and lax.ppermute only.
A program may use at most 64 MiB of HBM per device.

v0:
```python
import jax
import jax.numpy as jnp
from jax import lax
from jax.sharding import PartitionSpec as P


def partner_2(block, axis, distance):
    count = lax.axis_size(axis)
    route = []
    for low in range(count):
        high = low | 1 << distance
        if high != low and high < count:
            route += [(low, high), (high, low)]
    return lax.ppermute(block, axis, route)


def swap_level(values, bit_index):
    return partner_2(values, "srow", bit_index)


def swap_outer(values, bit_index):
    return partner_2(values, "srow", bit_index)


def sum_columns(values):
    return lax.psum_scatter(values, "scol", scatter_dimension=0, tiled=True)


def share_shape(buffer):
    return buffer.reshape((buffer.shape[0], 2, 2, 2, buffer.shape[1] // 8))


def halve_bit(shaped, bit_index, remaining, partner_swap):
    offset = lax.axis_index("srow")
    axis_place = (
        shaped.ndim - 1 - len(remaining) + len([other for other in remaining if other > bit_index])
    )
    own_bit = offset >> bit_index & 1
    kept_half = lax.dynamic_index_in_dim(shaped, own_bit, axis_place, keepdims=False)
    sent_half = lax.dynamic_index_in_dim(shaped, 1 - own_bit, axis_place, keepdims=False)
    return kept_half + partner_swap(sent_half, bit_index)


def halving(shaped, level_depth, partner_swap):
    remaining = [2, 1, 0]
    visiting = list(range(level_depth))
    for bit_index in visiting:
        shaped = halve_bit(shaped, bit_index, remaining, partner_swap)
        remaining = [other for other in remaining if other != bit_index]
    return shaped.reshape((shaped.shape[0], -1))


def place_shares(shaped, update_part, level_depth):
    offset = lax.axis_index("srow")
    anchor = offset * 0
    width = shaped.shape[-1]
    update_shaped = update_part.reshape(
        (update_part.shape[0],) + (2,) * (3 - level_depth) + (1,) * level_depth + (width,)
    )
    starts = [anchor] + [anchor] * (3 - level_depth)
    starts = starts + [offset >> 3 - place & 1 for place in range(4 - level_depth, 4)] + [anchor]
    current = lax.dynamic_slice(shaped, starts, update_shaped.shape)
    return lax.dynamic_update_slice(shaped, current + update_shaped, starts)


def gather_rows(stacked, level_depth):
    offset = lax.axis_index("srow")
    pieces = stacked[:, 0]
    for bit_index in range(level_depth):
        partner = partner_2(pieces, "srow", bit_index)
        lower_half = offset >> bit_index & 1 == 0
        pieces = jnp.where(
            lower_half,
            jnp.concatenate([pieces, partner], axis=0),
            jnp.concatenate([partner, pieces], axis=0),
        )
    return pieces


def apply_slot(whole_stack, slot, solution):
    matrix = whole_stack[:, slot, :].astype(jnp.float32)
    return jnp.dot(
        matrix, solution, precision=lax.Precision.HIGHEST, preferred_element_type=jnp.float32
    )


def solve_with(whole_stack, summed):
    return -apply_slot(whole_stack, 0, summed)


def shards(
    leaf_rhs, leaf_inverse, leaf_blocks, leaf_outer, leaf_targets, level_one, level_two, level_three
):
    weights = leaf_targets[0, 0].astype(jnp.bfloat16)
    leaf_solution = jnp.einsum(
        "jab,jbn->jan", leaf_inverse[0, 0], leaf_rhs[0, 0], preferred_element_type=jnp.float32
    ).astype(jnp.bfloat16)
    masked_blocks = leaf_blocks[0, 0] * weights[:, :3, None, None]
    level_terms = jnp.einsum(
        "jtab,jbn->tan", masked_blocks, leaf_solution, preferred_element_type=jnp.float32
    )
    masked_outer = leaf_outer[0, 0] * weights[:, 3, None, None]
    outer_buffer = jnp.einsum(
        "jab,jbn->an", masked_outer, leaf_solution, preferred_element_type=jnp.float32
    )
    stacks = [gather_rows(level_one, 1), gather_rows(level_two, 2), gather_rows(level_three, 3)]
    results = []
    buffers = [
        share_shape(level_terms[0]),
        share_shape(level_terms[1]),
        share_shape(level_terms[2]),
    ]
    outer_full = share_shape(outer_buffer)
    for level_depth in (1, 2, 3):
        whole_stack = stacks[level_depth - 1]
        solution = solve_with(
            whole_stack, halving(buffers[level_depth - 1], level_depth, swap_level)
        )
        results = results + [solution.astype(jnp.bfloat16)[:, None, :]]
        for target_level in range(level_depth, 4):
            update_part = apply_slot(whole_stack, target_level - level_depth + 1, solution)
            if target_level < 3:
                buffers[target_level] = place_shares(
                    buffers[target_level], update_part, level_depth
                )
            else:
                outer_full = place_shares(outer_full, update_part, level_depth)
    outer_update = sum_columns(halving(outer_full, 3, swap_outer))
    return (results[0], results[1], results[2], outer_update)


def solution(mesh):
    placed = (
        P("srow", "scol", None, None, None),
        P("srow", "scol", None, None, None),
        P("srow", "scol", None, None, None, None),
        P("srow", "scol", None, None, None),
        P("srow", "scol", None, None),
        P("srow", "scol", None, None),
        P("srow", "scol", None, None),
        P("srow", "scol", None, None),
    )
    return jax.shard_map(
        shards,
        mesh=mesh,
        in_specs=placed,
        out_specs=(
            P(None, "scol", "srow"),
            P(None, "scol", "srow"),
            P(None, "scol", "srow"),
            P("scol", "srow"),
        ),
        check_vma=False,
    )
```

profile of v0, /device:TPU:1, one launch (start us, length us, event | category | flops | bytes accessed | tf_op | source)
XLA Modules:
  0.0 184.2 jit_solution(15684123633732349687)
XLA Ops:
  7.2 0.8 convert_bitcast_fusion.3
  8.4 1.5 convolution_convert_fusion
  9.9 1.0 fusion.1
  10.9 1.2 fusion.22
  12.1 1.3 copy.53
  13.4 0.8 dynamic-slice_bitcast_fusion.3
  14.2 3.9 %collective-permute-start.1 = (f32[256,2,2,64]{0,3,2,1:T(8,128)}, f32[256,2,2,64]{0,3,2,1:T(8,128)}, u32[]{:S(2)}, u32[]{:S(2)}) collective-permute-start(f32[256,2,2,64]{0,3,2,1:T(8,128)} %dynamic-slice_bitcast_fusion.3), channel_id=1, source_target_pairs={{0,16},{16,0},{32,48},{48,32},{64,80},{80,64},{96,112},{112,96},{1... | collective-permute-start | bytes 786440 | tf_op jit(solution)/shard_map/ppermute | solution.py:14
  18.1 0.7 copy.80
  18.9 1.9 %collective-permute-start = (bf16[128,4,256]{2,0,1:T(8,128)(2,1)}, bf16[128,4,256]{2,0,1:T(8,128)(2,1)}, u32[]{:S(2)}, u32[]{:S(2)}) collective-permute-start(bf16[128,4,256]{2,0,1:T(8,128)(2,1)} %bitcast.193), channel_id=1, source_target_pairs={{0,16},{16,0},{32,48},{48,32},{64,80},{80,64},{96,112},{112,96},{1... | collective-permute-start | bytes 786440 | tf_op jit(solution)/shard_map/ppermute | solution.py:14
  20.8 3.4 %collective-permute-start.2 = (bf16[64,3,256]{2,0,1:T(8,128)(2,1)S(1)}, bf16[64,3,256]{2,0,1:T(8,128)(2,1)}, u32[]{:S(2)}, u32[]{:S(2)}) collective-permute-start(bf16[64,3,256]{2,0,1:T(8,128)(2,1)S(1)} %bitcast.213), channel_id=1, source_target_pairs={{0,16},{16,0},{32,48},{48,32},{64,80},{80,64},{96,112},{112,96},{1... | collective-permute-start | bytes 294920 | tf_op jit(solution)/shard_map/ppermute | solution.py:14
  24.2 0.8 copy.81
  24.9 1.9 %collective-permute-start.6 = (bf16[32,2,256]{2,0,1:T(8,128)(2,1)S(1)}, bf16[32,2,256]{2,0,1:T(8,128)(2,1)}, u32[]{:S(2)}, u32[]{:S(2)}) collective-permute-start(bf16[32,2,256]{2,0,1:T(8,128)(2,1)S(1)} %bitcast.211), channel_id=1, source_target_pairs={{0,16},{16,0},{32,48},{48,32},{64,80},{80,64},{96,112},{112,96},{1... | collective-permute-start | bytes 98312 | tf_op jit(solution)/shard_map/ppermute | solution.py:14
  27.1 1.2 copy.58
  28.4 0.9 copy.60
  29.2 1.3 copy.62
  30.5 0.9 maximum_select_fusion.5
  31.4 6.9 %collective-permute-start.7 = (bf16[64,2,256]{2,0,1:T(8,128)(2,1)S(1)}, bf16[64,2,256]{2,0,1:T(8,128)(2,1)S(1)}, u32[]{:S(2)}, u32[]{:S(2)}) collective-permute-start(bf16[64,2,256]{2,0,1:T(8,128)(2,1)S(1)} %maximum_select_fusion.5), channel_id=1, source_target_pairs={{0,32},{32,0},{16,48},{48,16},{64,96},{96,64},{80,112},{112,80},{1... | collective-permute-start | bytes 196616 | tf_op jit(solution)/shard_map/ppermute | solution.py:14
  38.5 1.5 collective-permute-done.7
  40.0 3.4 %collective-permute-start.8 = (bf16[128,2,256]{2,0,1:T(8,128)(2,1)S(1)}, bf16[128,2,256]{2,0,1:T(8,128)(2,1)S(1)}, u32[]{:S(2)}, u32[]{:S(2)}) collective-permute-start(bf16[128,2,256]{2,0,1:T(8,128)(2,1)S(1)} %maximum_select_fusion.4), channel_id=1, source_target_pairs={{0,64},{64,0},{16,80},{80,16},{32,96},{96,32},{48,112},{112,48},{1... | collective-permute-start | bytes 393224 | tf_op jit(solution)/shard_map/ppermute | solution.py:14
  43.4 1.1 bitcast_add_fusion.3
  44.5 1.3 maximum_select_fusion
  46.2 0.3 fusion.4
  46.6 3.2 %collective-permute-start.4 = (f32[256,2,2,64]{0,3,2,1:T(8,128)S(1)}, f32[256,2,2,64]{0,3,2,1:T(8,128)S(1)}, u32[]{:S(2)}, u32[]{:S(2)}) collective-permute-start(f32[256,2,2,64]{0,3,2,1:T(8,128)S(1)} %dynamic-slice_bitcast_fusion.2), channel_id=1, source_target_pairs={{0,16},{16,0},{32,48},{48,32},{64,80},{80,64},{96,112},{112,96},{1... | collective-permute-start | bytes 786440 | tf_op jit(solution)/shard_map/ppermute | solution.py:14
  49.9 1.0 maximum_select_fusion.3
  50.9 4.4 %collective-permute-start.3 = (bf16[128,3,256]{2,0,1:T(8,128)(2,1)S(1)}, bf16[128,3,256]{2,0,1:T(8,128)(2,1)S(1)}, u32[]{:S(2)}, u32[]{:S(2)}) collective-permute-start(bf16[128,3,256]{2,0,1:T(8,128)(2,1)S(1)} %maximum_select_fusion.3), channel_id=1, source_target_pairs={{0,32},{32,0},{16,48},{48,16},{64,96},{96,64},{80,112},{112,80},{1... | collective-permute-start | bytes 589832 | tf_op jit(solution)/shard_map/ppermute | solution.py:14
  55.3 0.3 fusion.5
  55.7 3.0 %collective-permute-start.5 = (f32[256,2,64]{0,2,1:T(8,128)S(1)}, f32[256,2,64]{0,2,1:T(8,128)S(1)}, u32[]{:S(2)}, u32[]{:S(2)}) collective-permute-start(f32[256,2,64]{0,2,1:T(8,128)S(1)} %dynamic-slice_bitcast_fusion.6), channel_id=1, source_target_pairs={{0,32},{32,0},{16,48},{48,16},{64,96},{96,64},{80,112},{112,80},{1... | collective-permute-start | bytes 393224 | tf_op jit(solution)/shard_map/ppermute | solution.py:14
  58.8 2.1 %collective-permute-done.3 = bf16[128,3,256]{2,0,1:T(8,128)(2,1)S(1)} collective-permute-done((bf16[128,3,256]{2,0,1:T(8,128)(2,1)S(1)}, bf16[128,3,256]{2,0,1:T(8,128)(2,1)S(1)}, u32[]{:S(2)}, u32[]{:S(2)}) %collective-permute-start.3) | collective-permute-done | bytes 196640 | tf_op jit(solution)/shard_map/ppermute | solution.py:14
  61.1 3.8 %collective-permute-done.5 = f32[256,2,64]{0,2,1:T(8,128)S(1)} collective-permute-done((f32[256,2,64]{0,2,1:T(8,128)S(1)}, f32[256,2,64]{0,2,1:T(8,128)S(1)}, u32[]{:S(2)}, u32[]{:S(2)}) %collective-permute-start.5) | collective-permute-done | bytes 131104 | tf_op jit(solution)/shard_map/ppermute | solution.py:14
  65.5 1.9 %collective-permute-start.9 = (f32[256,2,2,64]{0,3,1,2:T(8,128)S(1)}, f32[256,2,2,64]{0,3,1,2:T(8,128)S(1)}, u32[]{:S(2)}, u32[]{:S(2)}) collective-permute-start(f32[256,2,2,64]{0,3,1,2:T(8,128)S(1)} %dynamic-slice_bitcast_fusion.1), channel_id=1, source_target_pairs={{0,16},{16,0},{32,48},{48,32},{64,80},{80,64},{96,112},{112,96},{1... | collective-permute-start | bytes 786440 | tf_op jit(solution)/shard_map/ppermute | solution.py:14
  67.4 0.6 convolution_bitcast_fusion
  68.1 4.5 %collective-permute-done.9 = f32[256,2,2,64]{0,3,1,2:T(8,128)S(1)} collective-permute-done((f32[256,2,2,64]{0,3,1,2:T(8,128)S(1)}, f32[256,2,2,64]{0,3,1,2:T(8,128)S(1)}, u32[]{:S(2)}, u32[]{:S(2)}) %collective-permute-start.9) | collective-permute-done | bytes 262176 | tf_op jit(solution)/shard_map/ppermute | solution.py:14
  72.7 3.1 %collective-permute-start.10 = (f32[256,2,64]{0,2,1:T(8,128)S(1)}, f32[256,2,64]{0,2,1:T(8,128)S(1)}, u32[]{:S(2)}, u32[]{:S(2)}) collective-permute-start(f32[256,2,64]{0,2,1:T(8,128)S(1)} %dynamic-slice_bitcast_fusion.5), channel_id=1, source_target_pairs={{0,32},{32,0},{16,48},{48,16},{64,96},{96,64},{80,112},{112,80},{1... | collective-permute-start | bytes 393224 | tf_op jit(solution)/shard_map/ppermute | solution.py:14
  75.8 0.3 fusion.7
  76.2 4.3 %collective-permute-done.10 = f32[256,2,64]{0,2,1:T(8,128)S(1)} collective-permute-done((f32[256,2,64]{0,2,1:T(8,128)S(1)}, f32[256,2,64]{0,2,1:T(8,128)S(1)}, u32[]{:S(2)}, u32[]{:S(2)}) %collective-permute-start.10) | collective-permute-done | bytes 131104 | tf_op jit(solution)/shard_map/ppermute | solution.py:14
  80.6 2.6 %collective-permute-start.11 = (f32[256,64]{0,1:T(8,128)S(1)}, f32[256,64]{0,1:T(8,128)S(1)}, u32[]{:S(2)}, u32[]{:S(2)}) collective-permute-start(f32[256,64]{0,1:T(8,128)S(1)} %dynamic-slice_bitcast_fusion.8), channel_id=1, source_target_pairs={{0,64},{64,0},{16,80},{80,16},{32,96},{96,32},{48,112},{112,48},{1... | collective-permute-start | bytes 196616 | tf_op jit(solution)/shard_map/ppermute | solution.py:14
  83.5 2.1 %collective-permute-done.11 = f32[256,64]{0,1:T(8,128)S(1)} collective-permute-done((f32[256,64]{0,1:T(8,128)S(1)}, f32[256,64]{0,1:T(8,128)S(1)}, u32[]{:S(2)}, u32[]{:S(2)}) %collective-permute-start.11) | collective-permute-done | bytes 65568 | tf_op jit(solution)/shard_map/ppermute | solution.py:14
  86.2 1.9 %collective-permute-start.12 = (f32[256,2,2,64]{0,3,2,1:T(8,128)S(1)}, f32[256,2,2,64]{0,3,2,1:T(8,128)S(1)}, u32[]{:S(2)}, u32[]{:S(2)}) collective-permute-start(f32[256,2,2,64]{0,3,2,1:T(8,128)S(1)} %dynamic-slice_bitcast_fusion), channel_id=1, source_target_pairs={{0,16},{16,0},{32,48},{48,32},{64,80},{80,64},{96,112},{112,96},{1... | collective-permute-start | bytes 786440 | tf_op jit(solution)/shard_map/ppermute | solution.py:14
  88.1 5.2 %collective-permute-done.12 = f32[256,2,2,64]{0,3,2,1:T(8,128)S(1)} collective-permute-done((f32[256,2,2,64]{0,3,2,1:T(8,128)S(1)}, f32[256,2,2,64]{0,3,2,1:T(8,128)S(1)}, u32[]{:S(2)}, u32[]{:S(2)}) %collective-permute-start.12) | collective-permute-done | bytes 262176 | tf_op jit(solution)/shard_map/ppermute | solution.py:14
  93.3 4.3 %collective-permute-start.13 = (f32[256,2,64]{0,2,1:T(8,128)S(1)}, f32[256,2,64]{0,2,1:T(8,128)S(1)}, u32[]{:S(2)}, u32[]{:S(2)}) collective-permute-start(f32[256,2,64]{0,2,1:T(8,128)S(1)} %dynamic-slice_bitcast_fusion.4), channel_id=1, source_target_pairs={{0,32},{32,0},{16,48},{48,16},{64,96},{96,64},{80,112},{112,80},{1... | collective-permute-start | bytes 393224 | tf_op jit(solution)/shard_map/ppermute | solution.py:14
  97.7 0.8 copy.64
  98.5 2.1 %collective-permute-done.13 = f32[256,2,64]{0,2,1:T(8,128)S(1)} collective-permute-done((f32[256,2,64]{0,2,1:T(8,128)S(1)}, f32[256,2,64]{0,2,1:T(8,128)S(1)}, u32[]{:S(2)}, u32[]{:S(2)}) %collective-permute-start.13) | collective-permute-done | bytes 131104 | tf_op jit(solution)/shard_map/ppermute | solution.py:14
  100.6 2.8 %collective-permute-start.14 = (f32[256,64]{0,1:T(8,128)S(1)}, f32[256,64]{0,1:T(8,128)S(1)}, u32[]{:S(2)}, u32[]{:S(2)}) collective-permute-start(f32[256,64]{0,1:T(8,128)S(1)} %dynamic-slice_bitcast_fusion.7), channel_id=1, source_target_pairs={{0,64},{64,0},{16,80},{80,16},{32,96},{96,32},{48,112},{112,48},{1... | collective-permute-start | bytes 196616 | tf_op jit(solution)/shard_map/ppermute | solution.py:14
  103.5 0.7 copy.65
  104.2 1.4 collective-permute-done.14
  105.6 0.7 copy.73
  106.4 0.6 convert_bitcast_fusion.2
  107.0 70.3 %reduce-scatter.4.cloned.1.call-done = f32[16,64]{1,0:T(8,128)} async-done(((f32[256,64]{1,0:T(8,128)}), f32[16,64]{1,0:T(8,128)}) %reduce-scatter.4.cloned.1.call-update) | async-done | bytes 4112
  (54 shorter events, 3.3 us)
Async XLA Ops:
  7.2 1.2 copy-start
  7.2 170.2 %reduce-scatter.4.cloned.1.call-start = ((), (), s32[]{:S(2)}) async-start(), calls=%async_computation.1 | async-start | bytes 139264
  7.2 2.7 %copy-start.6 = (bf16[1,1,4,3,256,256]{5,4,3,2,1,0:T(8,128)(2,1)S(1)}, bf16[1,1,4,3,256,256]{5,4,3,2,1,0:T(8,128)(2,1)}, u32[]{:S(2)}) copy-start(bf16[1,1,4,3,256,256]{5,4,3,2,1,0:T(8,128)(2,1)} %param.10) | copy-start | bytes 4718596
  12.1 6.1 %copy-start.4 = (bf16[128,1,4,256]{3,2,1,0:T(4,128)(2,1)S(1)}, bf16[128,1,4,256]{3,2,1,0:T(4,128)(2,1)}, u32[]{:S(2)}) copy-start(bf16[128,1,4,256]{3,2,1,0:T(4,128)(2,1)} %param.13) | copy-start | bytes 786436
  12.1 8.7 %copy-start.5 = (bf16[64,1,3,256]{3,0,2,1:T(8,128)(2,1)S(1)}, bf16[64,1,3,256]{3,0,2,1:T(8,128)(2,1)}, u32[]{:S(2)}) copy-start(bf16[64,1,3,256]{3,0,2,1:T(8,128)(2,1)} %param.14) | copy-start | bytes 294916
  13.4 13.5 %copy-start.2 = (f32[1,256,512]{1,2,0:T(8,128)}, f32[1,256,512]{1,2,0:T(8,128)S(1)}, u32[]{:S(2)}) copy-start(f32[1,256,512]{1,2,0:T(8,128)S(1)} %copy.53) | copy-start | bytes 1572868
  14.2 29.2 %collective-permute-start.1 = (f32[256,2,2,64]{0,3,2,1:T(8,128)}, f32[256,2,2,64]{0,3,2,1:T(8,128)}, u32[]{:S(2)}, u32[]{:S(2)}) collective-permute-start(f32[256,2,2,64]{0,3,2,1:T(8,128)} %dynamic-slice_bitcast_fusion.3), channel_id=1, source_target_pairs={{0,16},{16,0},{32,48},{48,32},{64,80},{80,64},{96,112},{112,96},{1... | collective-permute-start | bytes 786440 | tf_op jit(solution)/shard_map/ppermute | solution.py:14
  18.9 25.6 %collective-permute-start = (bf16[128,4,256]{2,0,1:T(8,128)(2,1)}, bf16[128,4,256]{2,0,1:T(8,128)(2,1)}, u32[]{:S(2)}, u32[]{:S(2)}) collective-permute-start(bf16[128,4,256]{2,0,1:T(8,128)(2,1)} %bitcast.193), channel_id=1, source_target_pairs={{0,16},{16,0},{32,48},{48,32},{64,80},{80,64},{96,112},{112,96},{1... | collective-permute-start | bytes 786440 | tf_op jit(solution)/shard_map/ppermute | solution.py:14
  20.8 29.0 %collective-permute-start.2 = (bf16[64,3,256]{2,0,1:T(8,128)(2,1)S(1)}, bf16[64,3,256]{2,0,1:T(8,128)(2,1)}, u32[]{:S(2)}, u32[]{:S(2)}) collective-permute-start(bf16[64,3,256]{2,0,1:T(8,128)(2,1)S(1)} %bitcast.213), channel_id=1, source_target_pairs={{0,16},{16,0},{32,48},{48,32},{64,80},{80,64},{96,112},{112,96},{1... | collective-permute-start | bytes 294920 | tf_op jit(solution)/shard_map/ppermute | solution.py:14
  24.9 5.6 %collective-permute-start.6 = (bf16[32,2,256]{2,0,1:T(8,128)(2,1)S(1)}, bf16[32,2,256]{2,0,1:T(8,128)(2,1)}, u32[]{:S(2)}, u32[]{:S(2)}) collective-permute-start(bf16[32,2,256]{2,0,1:T(8,128)(2,1)S(1)} %bitcast.211), channel_id=1, source_target_pairs={{0,16},{16,0},{32,48},{48,32},{64,80},{80,64},{96,112},{112,96},{1... | collective-permute-start | bytes 98312 | tf_op jit(solution)/shard_map/ppermute | solution.py:14
  31.4 8.6 %collective-permute-start.7 = (bf16[64,2,256]{2,0,1:T(8,128)(2,1)S(1)}, bf16[64,2,256]{2,0,1:T(8,128)(2,1)S(1)}, u32[]{:S(2)}, u32[]{:S(2)}) collective-permute-start(bf16[64,2,256]{2,0,1:T(8,128)(2,1)S(1)} %maximum_select_fusion.5), channel_id=1, source_target_pairs={{0,32},{32,0},{16,48},{48,16},{64,96},{96,64},{80,112},{112,80},{1... | collective-permute-start | bytes 196616 | tf_op jit(solution)/shard_map/ppermute | solution.py:14
  40.0 28.0 %collective-permute-start.8 = (bf16[128,2,256]{2,0,1:T(8,128)(2,1)S(1)}, bf16[128,2,256]{2,0,1:T(8,128)(2,1)S(1)}, u32[]{:S(2)}, u32[]{:S(2)}) collective-permute-start(bf16[128,2,256]{2,0,1:T(8,128)(2,1)S(1)} %maximum_select_fusion.4), channel_id=1, source_target_pairs={{0,64},{64,0},{16,80},{80,16},{32,96},{96,32},{48,112},{112,48},{1... | collective-permute-start | bytes 393224 | tf_op jit(solution)/shard_map/ppermute | solution.py:14
  46.6 12.2 %copy-start.1 = (f32[256,2,2,2,64]{0,4,1,3,2:T(8,128)S(1)}, f32[256,2,2,2,64]{0,4,1,3,2:T(8,128)}, u32[]{:S(2)}) copy-start(f32[256,2,2,2,64]{0,4,1,3,2:T(8,128)} %copy.60) | copy-start | bytes 1572868
  46.6 9.0 %collective-permute-start.4 = (f32[256,2,2,64]{0,3,2,1:T(8,128)S(1)}, f32[256,2,2,64]{0,3,2,1:T(8,128)S(1)}, u32[]{:S(2)}, u32[]{:S(2)}) collective-permute-start(f32[256,2,2,64]{0,3,2,1:T(8,128)S(1)} %dynamic-slice_bitcast_fusion.2), channel_id=1, source_target_pairs={{0,16},{16,0},{32,48},{48,32},{64,80},{80,64},{96,112},{112,96},{1... | collective-permute-start | bytes 786440 | tf_op jit(solution)/shard_map/ppermute | solution.py:14
  50.9 10.0 %collective-permute-start.3 = (bf16[128,3,256]{2,0,1:T(8,128)(2,1)S(1)}, bf16[128,3,256]{2,0,1:T(8,128)(2,1)S(1)}, u32[]{:S(2)}, u32[]{:S(2)}) collective-permute-start(bf16[128,3,256]{2,0,1:T(8,128)(2,1)S(1)} %maximum_select_fusion.3), channel_id=1, source_target_pairs={{0,32},{32,0},{16,48},{48,16},{64,96},{96,64},{80,112},{112,80},{1... | collective-permute-start | bytes 589832 | tf_op jit(solution)/shard_map/ppermute | solution.py:14
  55.7 11.7 %copy-start.3 = (bf16[512,256,4]{1,0,2:T(8,128)(2,1)S(1)}, bf16[512,256,4]{1,0,2:T(8,128)(2,1)}, u32[]{:S(2)}) copy-start(bf16[512,256,4]{1,0,2:T(8,128)(2,1)} %copy.62) | copy-start | bytes 3145732
  55.7 11.7 %copy-start.7 = (bf16[1,1,4,256,256]{4,3,2,1,0:T(8,128)(2,1)S(1)}, bf16[1,1,4,256,256]{4,3,2,1,0:T(8,128)(2,1)}, u32[]{:S(2)}) copy-start(bf16[1,1,4,256,256]{4,3,2,1,0:T(8,128)(2,1)} %param.11) | copy-start | bytes 1572868
  55.7 9.1 %collective-permute-start.5 = (f32[256,2,64]{0,2,1:T(8,128)S(1)}, f32[256,2,64]{0,2,1:T(8,128)S(1)}, u32[]{:S(2)}, u32[]{:S(2)}) collective-permute-start(f32[256,2,64]{0,2,1:T(8,128)S(1)} %dynamic-slice_bitcast_fusion.6), channel_id=1, source_target_pairs={{0,32},{32,0},{16,48},{48,16},{64,96},{96,64},{80,112},{112,80},{1... | collective-permute-start | bytes 393224 | tf_op jit(solution)/shard_map/ppermute | solution.py:14
  65.5 7.1 %collective-permute-start.9 = (f32[256,2,2,64]{0,3,1,2:T(8,128)S(1)}, f32[256,2,2,64]{0,3,1,2:T(8,128)S(1)}, u32[]{:S(2)}, u32[]{:S(2)}) collective-permute-start(f32[256,2,2,64]{0,3,1,2:T(8,128)S(1)} %dynamic-slice_bitcast_fusion.1), channel_id=1, source_target_pairs={{0,16},{16,0},{32,48},{48,32},{64,80},{80,64},{96,112},{112,96},{1... | collective-permute-start | bytes 786440 | tf_op jit(solution)/shard_map/ppermute | solution.py:14
  72.7 7.8 %collective-permute-start.10 = (f32[256,2,64]{0,2,1:T(8,128)S(1)}, f32[256,2,64]{0,2,1:T(8,128)S(1)}, u32[]{:S(2)}, u32[]{:S(2)}) collective-permute-start(f32[256,2,64]{0,2,1:T(8,128)S(1)} %dynamic-slice_bitcast_fusion.5), channel_id=1, source_target_pairs={{0,32},{32,0},{16,48},{48,16},{64,96},{96,64},{80,112},{112,80},{1... | collective-permute-start | bytes 393224 | tf_op jit(solution)/shard_map/ppermute | solution.py:14
  80.6 5.0 %collective-permute-start.11 = (f32[256,64]{0,1:T(8,128)S(1)}, f32[256,64]{0,1:T(8,128)S(1)}, u32[]{:S(2)}, u32[]{:S(2)}) collective-permute-start(f32[256,64]{0,1:T(8,128)S(1)} %dynamic-slice_bitcast_fusion.8), channel_id=1, source_target_pairs={{0,64},{64,0},{16,80},{80,16},{32,96},{96,32},{48,112},{112,48},{1... | collective-permute-start | bytes 196616 | tf_op jit(solution)/shard_map/ppermute | solution.py:14
  86.2 7.1 %collective-permute-start.12 = (f32[256,2,2,64]{0,3,2,1:T(8,128)S(1)}, f32[256,2,2,64]{0,3,2,1:T(8,128)S(1)}, u32[]{:S(2)}, u32[]{:S(2)}) collective-permute-start(f32[256,2,2,64]{0,3,2,1:T(8,128)S(1)} %dynamic-slice_bitcast_fusion), channel_id=1, source_target_pairs={{0,16},{16,0},{32,48},{48,32},{64,80},{80,64},{96,112},{112,96},{1... | collective-permute-start | bytes 786440 | tf_op jit(solution)/shard_map/ppermute | solution.py:14
  93.3 7.2 %collective-permute-start.13 = (f32[256,2,64]{0,2,1:T(8,128)S(1)}, f32[256,2,64]{0,2,1:T(8,128)S(1)}, u32[]{:S(2)}, u32[]{:S(2)}) collective-permute-start(f32[256,2,64]{0,2,1:T(8,128)S(1)} %dynamic-slice_bitcast_fusion.4), channel_id=1, source_target_pairs={{0,32},{32,0},{16,48},{48,16},{64,96},{96,64},{80,112},{112,80},{1... | collective-permute-start | bytes 393224 | tf_op jit(solution)/shard_map/ppermute | solution.py:14
  100.6 5.0 %collective-permute-start.14 = (f32[256,64]{0,1:T(8,128)S(1)}, f32[256,64]{0,1:T(8,128)S(1)}, u32[]{:S(2)}, u32[]{:S(2)}) collective-permute-start(f32[256,64]{0,1:T(8,128)S(1)} %dynamic-slice_bitcast_fusion.7), channel_id=1, source_target_pairs={{0,64},{64,0},{16,80},{80,16},{32,96},{96,32},{48,112},{112,48},{1... | collective-permute-start | bytes 196616 | tf_op jit(solution)/shard_map/ppermute | solution.py:14
Sparse Core Ops, SparseCore 0:
  106.5 70.7 reduce-scatter.3
where the time goes:
time: 187 us; the launch traced here: 184 us
  waiting for transfers between devices  97.3 us (52%)
  starting transfers between devices  48.9 us (26%)
  between operations  14.6 us (8%)
  local copies, waits for them, and re-layouts  11.3 us (6%)
  other arithmetic  6.22 us (3%)
  matrix products  5.87 us (3%)
    unnamed x2, waiting for transfers between devices  70.3 us
    ppermute x15, starting transfers between devices, partner_2(): return lax.ppermute(block, axis, route)  48.8 us
    ppermute x15, waiting for transfers between devices, partner_2(): return lax.ppermute(block, axis, route)  27 us
    unnamed x21, local copies, waits for them, and re-layouts  4.11 us
  transfers between devices with their start and end apart: 16, of which 10 were waited for; matrix products, arithmetic and copies ran while one was open for 8% of the time, Pallas kernels for 0%

commit v1 on v0

v1 whole, which is shorter than its diff:
```python
import jax
import jax.numpy as jnp
from jax import lax
from jax.experimental import pallas as pl
from jax.experimental.pallas import tpu as pltpu
from jax.sharding import PartitionSpec as P

F32 = jnp.float32
BF16 = jnp.bfloat16
LEAF_BYTES = 12 << 20
TRANSFORM_BYTES = 6 << 20
SMALL_BYTES = 4 << 20
GROUPS_8 = [[g * 8 + i for i in range(8)] for g in range(4)]
GROUPS_4 = [[g * 4 + i for i in range(4)] for g in range(8)]


def in_vmem(x):
    return pltpu.with_memory_space_constraint(x, pltpu.VMEM)


def in_hbm(x):
    return pltpu.with_memory_space_constraint(x, pltpu.HBM)


def dot(a, b):
    return jnp.dot(a, b, preferred_element_type=F32)


def dot_wide(a, b):
    high = b.astype(BF16)
    low = (b - high.astype(F32)).astype(BF16)
    return dot(a, high) + dot(a, low)


def low_lanes(shape):
    return lax.broadcasted_iota(jnp.int32, shape, 1) < 64


def join_halves(first, second, upper):
    low = low_lanes(first.shape)
    if upper:
        return jnp.where(low, pltpu.roll(first, 64, 1), second)
    return jnp.where(low, first, pltpu.roll(second, 64, 1))


def tile(ref, t):
    return ref[:, t * 128 : (t + 1) * 128]


def leaf_kernel(
    w_ref, inv_hbm, rhs_hbm, blk_hbm, out_hbm,
    t1_ref, t2_ref, t3_ref, o_ref, sent_ref,
    inv, rhs, blk, out, y, masked, sems,
):
    copies = []
    for j in range(4):
        pairs = ((inv_hbm, inv), (rhs_hbm, rhs), (blk_hbm, blk), (out_hbm, out))
        copies.append([pltpu.make_async_copy(a.at[j], b.at[j], sems.at[j, i]) for i, (a, b) in enumerate(pairs)])
    for first in (0, 2):
        for j in range(4):
            for copy in copies[j][first : first + 2]:
                copy.start()
    for j in range(4):
        copies[j][0].wait()
        copies[j][1].wait()
        y[j * 256 : (j + 1) * 256, :] = dot(inv[j], rhs[j]).astype(BF16)
    for j in range(4):
        copies[j][2].wait()
        copies[j][3].wait()
        for t in range(4):
            block = blk[j, t] if t < 3 else out[j]
            masked[t, :, j * 256 : (j + 1) * 256] = block * w_ref[j, t].astype(F32).astype(BF16)
    for t, into in enumerate((t1_ref, t2_ref, t3_ref, o_ref)):
        into[...] = dot(masked[t], y[...]).astype(into.dtype)
    for half in range(2):
        sent_ref[:, half * 128 : (half + 1) * 128] = own_and_other(t1_ref, half)[1].astype(BF16)


def own_and_other(t1_ref, half):
    first, second = tile(t1_ref, 2 * half).astype(F32), tile(t1_ref, 2 * half + 1).astype(F32)
    even = join_halves(first, second, False)
    odd = join_halves(first, second, True)
    own_upper = (lax.axis_index("srow") & 1) == 1
    return jnp.where(own_upper, odd, even), jnp.where(own_upper, even, odd)


def leaf_terms(weights, inverse, rhs, blocks, outer):
    full = pltpu.VMEM((256, 512), F32)
    return pl.pallas_call(
        leaf_kernel,
        name="leaf",
        in_specs=[pl.BlockSpec(memory_space=pltpu.SMEM)] + [pl.BlockSpec(memory_space=pl.ANY)] * 4,
        out_shape=[pltpu.VMEM((256, 512), BF16), full, full, full, pltpu.VMEM((256, 256), BF16)],
        scratch_shapes=[
            pltpu.VMEM((4, 256, 256), BF16),
            pltpu.VMEM((4, 256, 512), BF16),
            pltpu.VMEM((4, 3, 256, 256), BF16),
            pltpu.VMEM((4, 256, 256), BF16),
            pltpu.VMEM((1024, 512), BF16),
            pltpu.VMEM((4, 256, 1024), BF16),
            pltpu.SemaphoreType.DMA((4, 4)),
        ],
        compiler_params=pltpu.CompilerParams(vmem_limit_bytes=LEAF_BYTES),
        cost_estimate=pl.CostEstimate(flops=1_342_177_280, bytes_accessed=6_000_000, transcendentals=0),
    )(in_hbm(weights), in_hbm(inverse), in_hbm(rhs), in_hbm(blocks), in_hbm(outer))


def first_kernel(t1_ref, t2_ref, t3_ref, o_ref, m1_ref, m1r_ref, t2n_ref, t3n_ref, on_ref, d1_ref, one):
    row = lax.axis_index("srow")
    own = pl.multiple_of((row & 1) * 128, 128)
    other = pl.multiple_of(128 - (row & 1) * 128, 128)
    for slot in range(4):
        into = d1_ref if slot == 0 else one.at[slot - 1]
        into[pl.ds(own, 128), :] = m1_ref[:, slot, :]
        into[pl.ds(other, 128), :] = m1r_ref[:, slot, :]
    x1 = dot(d1_ref[...], t1_ref[...]).astype(BF16)
    under = dot(one[...].reshape(768, 256), x1)
    t2n_ref[...] = t2_ref[...] - under[:256]
    t3n_ref[...] = t3_ref[...] - under[256:512]
    on_ref[...] = o_ref[...] - under[512:]


def first_level(t1, t2, t3, o, m1, m1r):
    full = pltpu.VMEM((256, 512), F32)
    return pl.pallas_call(
        first_kernel,
        name="first",
        out_shape=[full, full, full, pltpu.VMEM((256, 256), BF16)],
        scratch_shapes=[pltpu.VMEM((3, 256, 256), BF16)],
        input_output_aliases={1: 0, 2: 1, 3: 2},
        compiler_params=pltpu.CompilerParams(vmem_limit_bytes=TRANSFORM_BYTES),
        cost_estimate=pl.CostEstimate(flops=5_000_000_000, bytes_accessed=3_000_000, transcendentals=0),
    )(*map(in_vmem, (t1, t2, t3, o, m1, m1r)))


def second_kernel(t2_ref, t3_ref, o_ref, m2_ref, m3_ref, a8_ref, d2_ref, two):
    for q in range(4):
        for slot in range(3):
            into = d2_ref if slot == 0 else two.at[slot - 1]
            into[q * 64 : (q + 1) * 64, :] = m2_ref[q, slot]
    t2 = t2_ref[...]
    x2 = dot(d2_ref[...], t2.astype(BF16)).astype(BF16)
    above = dot(two[...].reshape(512, 256), x2)
    t3 = t3_ref[...] - above[:256]
    o = o_ref[...] - above[256:]
    for k in range(8):
        cut = slice(k // 2 * 128, k // 2 * 128 + 128)
        odd = k % 2 == 1
        a8_ref[k, :256] = join_halves(t3[:, cut], o[:, cut], odd).astype(BF16)
        a8_ref[k, 256:384] = join_halves(t2[:128, cut], t2[128:, cut], odd).astype(BF16)
        for slot in range(2):
            for side in range(2):
                start = 384 + side * 64 + slot * 32
                a8_ref[k, start : start + 32] = m3_ref[:, slot, side * 128 : (side + 1) * 128]


def second_level(t2, t3, o, m2, m3):
    return pl.pallas_call(
        second_kernel,
        name="second",
        out_shape=[jax.ShapeDtypeStruct((8, 512, 128), BF16), pltpu.VMEM((256, 256), BF16)],
        scratch_shapes=[pltpu.VMEM((2, 256, 256), BF16)],
        compiler_params=pltpu.CompilerParams(vmem_limit_bytes=TRANSFORM_BYTES),
        cost_estimate=pl.CostEstimate(flops=200_000_000, bytes_accessed=3_000_000, transcendentals=0),
    )(*map(in_vmem, (t2, t3, o, m2, m3)))


def third_kernel(r8_ref, *rest):
    x3_ref, out_ref, own2_ref, sent2_ref, d3, l3, v = rest[-7:]
    total = r8_ref[0, :256].astype(F32)
    for k in range(1, 8):
        total = total + r8_ref[k, :256].astype(F32)
    for k in range(8):
        for side in range(2):
            cut = slice(side * 128, (side + 1) * 128)
            start = 384 + side * 64
            d3[k * 32 : (k + 1) * 32, cut] = r8_ref[k, start : start + 32]
            l3[k * 32 : (k + 1) * 32, cut] = r8_ref[k, start + 32 : start + 64]
    x3 = -dot_wide(d3[...], total)
    x3_ref[...] = jnp.transpose(x3)[:64, :].astype(BF16)
    v[...] = total + pltpu.roll(dot_wide(l3[...], x3), 64, 1)
    low = low_lanes((8, 128))
    for p in range(16):
        upper, lower = v[p * 16 : p * 16 + 8, :], v[p * 16 + 8 : p * 16 + 16, :]
        out_ref[p] = jnp.where(low, pltpu.roll(upper, 64, 1), lower).astype(BF16)
    sums = []
    for quad in range(2):
        folded = r8_ref[4 * quad, 256:384].astype(F32)
        for k in range(1, 4):
            folded = folded + r8_ref[4 * quad + k, 256:384].astype(F32)
        sums.append(folded)
    in_second = ((lax.axis_index("srow") >> 2) & 1) == 1
    own, other = jnp.where(in_second, sums[1], sums[0]), jnp.where(in_second, sums[0], sums[1])
    own2_ref[...] = own
    sent2_ref[...] = other.astype(BF16)


def third_level(r8, *after):
    return pl.pallas_call(
        third_kernel,
        name="third",
        in_specs=[pl.BlockSpec(memory_space=pltpu.VMEM)] + [pl.BlockSpec(memory_space=pl.ANY)] * len(after),
        out_shape=[
            jax.ShapeDtypeStruct((64, 256), BF16),
            pltpu.VMEM((16, 8, 128), BF16),
            pltpu.VMEM((128, 128), F32),
            pltpu.VMEM((128, 128), BF16),
        ],
        scratch_shapes=[pltpu.VMEM((256, 256), BF16), pltpu.VMEM((256, 256), BF16), pltpu.VMEM((256, 128), F32)],
        compiler_params=pltpu.CompilerParams(vmem_limit_bytes=SMALL_BYTES),
        cost_estimate=pl.CostEstimate(flops=70_000_000, bytes_accessed=1_300_000, transcendentals=0),
    )(in_vmem(r8), *after)


def lower_kernel(t1_ref, came1_ref, own2_ref, came2_ref, d1_ref, d2_ref, x1_ref, x2_ref):
    kept_one = jnp.concatenate([own_and_other(t1_ref, half)[0] for half in range(2)], axis=1)
    sum_one = kept_one + came1_ref[...].astype(F32)
    x1_ref[...] = (-dot_wide(d1_ref[...], sum_one)).astype(BF16)
    own, came = own2_ref[...], came2_ref[...].astype(F32)
    in_second = ((lax.axis_index("srow") >> 2) & 1) == 1
    first, second = jnp.where(in_second, came, own), jnp.where(in_second, own, came)
    sum_two = jnp.concatenate([join_halves(first, second, False), join_halves(first, second, True)], axis=0)
    x2_ref[...] = (-dot_wide(d2_ref[...], sum_two)).astype(BF16)


def lower_levels(t1, came1, own2, came2, d1, d2):
    return pl.pallas_call(
        lower_kernel,
        name="lower",
        out_shape=[jax.ShapeDtypeStruct((256, 256), BF16), jax.ShapeDtypeStruct((256, 128), BF16)],
        compiler_params=pltpu.CompilerParams(vmem_limit_bytes=SMALL_BYTES),
        cost_estimate=pl.CostEstimate(flops=1, bytes_accessed=1, transcendentals=0),
    )(*map(in_vmem, (t1, came1, own2, came2, d1, d2)))


def final_kernel(r_ref, after_ref, out_ref):
    total = r_ref[0].astype(F32)
    for k in range(1, 16):
        total = total + r_ref[k].astype(F32)
    out_ref[0:8, :] = total[:, :64]
    out_ref[8:16, :] = pltpu.roll(total, 64, 1)[:, :64]


def final_sum(received, after):
    return pl.pallas_call(
        final_kernel,
        name="final",
        in_specs=[pl.BlockSpec(memory_space=pltpu.VMEM), pl.BlockSpec(memory_space=pl.ANY)],
        out_shape=jax.ShapeDtypeStruct((16, 64), F32),
        compiler_params=pltpu.CompilerParams(vmem_limit_bytes=SMALL_BYTES),
        cost_estimate=pl.CostEstimate(flops=20_000, bytes_accessed=40_000, transcendentals=0),
    )(in_vmem(received), in_hbm(after))


def swap(block, flip):
    return lax.ppermute(block, "srow", [(i, i ^ flip) for i in range(32)])


def shards(
    leaf_rhs, leaf_inverse, leaf_blocks, leaf_outer, leaf_targets, level_one, level_two, level_three
):
    m1, m3 = level_one[:, 0], level_three[:, 0]
    m1r = swap(m1, 1)
    m2 = jnp.broadcast_to(jnp.transpose(level_two[:, 0], (1, 0, 2)), (4, 3, 64, 256))
    m2 = lax.all_to_all(m2, "srow", 0, 0, axis_index_groups=GROUPS_4, tiled=True)
    t1, t2, t3, o, sent1 = leaf_terms(
        leaf_targets[0, 0], leaf_inverse[0, 0], leaf_rhs[0, 0], leaf_blocks[0, 0], leaf_outer[0, 0]
    )
    came1 = swap(sent1, 1)
    t2, t3, o, d1 = first_level(t1, t2, t3, o, m1, m1r)
    a8, d2 = second_level(t2, t3, o, m2, m3)
    r8 = lax.all_to_all(a8, "srow", 0, 0, axis_index_groups=GROUPS_8, tiled=True)
    x3, parts, own2, sent2 = third_level(r8)
    received = lax.all_to_all(parts, "scol", 0, 0, tiled=True)
    x1, x2 = lower_levels(t1, came1, own2, swap(sent2, 4), d1, d2)
    outer_update = final_sum(received, x2)
    return (x1[:, None, :], x2[:, None, :], jnp.transpose(x3)[:, None, :], outer_update)


def solution(mesh):
    placed = (
        P("srow", "scol", None, None, None),
        P("srow", "scol", None, None, None),
        P("srow", "scol", None, None, None, None),
        P("srow", "scol", None, None, None),
        P("srow", "scol", None, None),
        P("srow", "scol", None, None),
        P("srow", "scol", None, None),
        P("srow", "scol", None, None),
    )
    return jax.shard_map(
        shards,
        mesh=mesh,
        in_specs=placed,
        out_specs=(
            P(None, "scol", "srow"),
            P(None, "scol", "srow"),
            P(None, "scol", "srow"),
            P("scol", "srow"),
        ),
        check_vma=False,
    )
```

time: 187 us -> 58.9 us (0.31); the launches traced: 184 us -> 58.5 us
  waiting for transfers between devices: 97.3 us -> 9.92 us
  between operations: 14.6 us -> 0.7 us
  starting transfers between devices: 48.9 us -> 35.4 us
  Pallas kernels: 0 us -> 10.8 us
  local copies, waits for them, and re-layouts: 11.3 us -> 1.68 us
  other arithmetic: 6.22 us -> 0 us
  matrix products: 5.87 us -> 0 us
    unnamed x2 -> x0, waiting for transfers between devices: 70.3 us -> none
    ppermute x15 -> x3, starting transfers between devices: 48.8 us -> 10.4 us  [swap(): return lax.ppermute(block, 'srow', [(i, i ^ flip) for i in range(32)])]
    ppermute x15 -> x3, waiting for transfers between devices: 27 us -> 1.84 us  [swap(): return lax.ppermute(block, 'srow', [(i, i ^ flip) for i in range(32)])]
    all_to_all x0 -> x3, starting transfers between devices: none -> 24.9 us  [the longest x1 16.5 us: shards(): received = lax.all_to_all(parts, 'scol', 0, 0, tiled=True)]
    pallas_call x0 -> x6, Pallas kernels: none -> 10.8 us  [the longest x1 4.33 us: leaf_terms(): pl.pallas_call(leaf_kernel, name='leaf', in_specs=[pl.BlockSpec(memory_sp...]
    all_to_all x0 -> x3, waiting for transfers between devices: none -> 8.08 us  [the longest x1 6.22 us: shards(): lax.all_to_all(a8, 'srow', 0, 0, axis_index_groups=GROUPS_8, tiled=True)]
    dot_general x12 -> x0, matrix products: 5.87 us -> none  [the longest x9 2.84 us: apply_slot(): jnp.dot(matrix, solution, precision=lax.Precision.HIGHEST, preferred_elem...]
    unnamed x21 -> x4, local copies, waits for them, and re-layouts: 4.11 us -> 0.01 us
  transfers between devices with their start and end apart: 16 -> 6, of which waited for: 10 -> 4; matrix products, arithmetic and copies ran while one was open for 8% -> 3% of each run, Pallas kernels for 0% -> 14%
where the time goes in v1:
time: 58.9 us; the launch traced here: 58.5 us
  starting transfers between devices  35.4 us (60%)
  Pallas kernels  10.8 us (18%)
  waiting for transfers between devices  9.92 us (17%)
  local copies, waits for them, and re-layouts  1.68 us (3%)
  between operations  0.7 us (1%)
    all_to_all x1, starting transfers between devices, shards(): received = lax.all_to_all(parts, 'scol', 0, 0, tiled=True)  16.5 us
    ppermute x3, starting transfers between devices, swap(): return lax.ppermute(block, 'srow', [(i, i ^ flip) for i in range(32)])  10.4 us
    all_to_all x1, waiting for transfers between devices, shards(): lax.all_to_all(a8, 'srow', 0, 0, axis_index_groups=GROUPS_8, tiled=True)  6.22 us
    all_to_all x1, starting transfers between devices, shards(): lax.all_to_all(a8, 'srow', 0, 0, axis_index_groups=GROUPS_8, tiled=True)  4.72 us
    pallas_call x1, Pallas kernels, leaf_terms(): pl.pallas_call(leaf_kernel, name='leaf', in_specs=[pl.BlockSpec(memory_sp...  4.33 us
    all_to_all x1, starting transfers between devices, shards(): lax.all_to_all(m2, 'srow', 0, 0, axis_index_groups=GROUPS_4, tiled=True)  3.72 us
    pallas_call x1, Pallas kernels, second_level(): pl.pallas_call(second_kernel, name='second', out_shape=[jax.ShapeDtypeStr...  2.13 us
    ppermute x3, waiting for transfers between devices, swap(): return lax.ppermute(block, 'srow', [(i, i ^ flip) for i in range(32)])  1.84 us
  transfers between devices with their start and end apart: 6, of which 4 were waited for; matrix products, arithmetic and copies ran while one was open for 3% of the time, Pallas kernels for 14%

profile of v1, /device:TPU:1, one launch (start us, length us, event | category | flops | bytes accessed | tf_op | source)
XLA Modules:
  0.0 58.5 jit_solution(2855719026646088399)
XLA Ops:
  0.6 4.0 %collective-permute-start.1 = (bf16[128,4,256]{2,1,0:T(4,128)(2,1)}, bf16[128,4,256]{2,1,0:T(4,128)(2,1)S(1)}, u32[]{:S(2)}, u32[]{:S(2)}) collective-permute-start(bf16[128,4,256]{2,1,0:T(4,128)(2,1)} %bitcast.16), channel_id=1, source_target_pairs={{0,16},{16,0},{32,48},{48,32},{64,80},{80,64},{96,112},{112,96},{1... | collective-permute-start | bytes 786440 | tf_op jit(solution)/shard_map/ppermute | solution.py:256
  4.6 1.7 %broadcast_in_dim.12 = bf16[4,3,64,256]{3,2,1,0:T(8,128)(2,1)} broadcast(bf16[3,64,256]{2,1,0:T(8,128)(2,1)} %bitcast.18), dimensions={1,2,3} | broadcast | bytes 491520 | tf_op jit(solution)/shard_map/broadcast_in_dim | solution.py:264
  6.3 3.7 %all-to-all-start = ((bf16[4,3,64,256]{3,2,1,0:T(8,128)(2,1)}), bf16[4,3,64,256]{3,2,1,0:T(8,128)(2,1)S(1)}, u32[]{:S(2)}, u32[]{:S(2)}) async-start(bf16[4,3,64,256]{3,2,1,0:T(8,128)(2,1)} %broadcast_in_dim.12), calls=%async_computation | async-start | bytes 786432 | tf_op jit(solution)/shard_map/all_to_all | solution.py:265
  10.0 0.0 copy-start.1
  10.0 4.3 %leaf.1 = (bf16[256,512]{1,0:T(8,128)(2,1)S(1)}, f32[256,512]{1,0:T(8,128)S(1)}, f32[256,512]{1,0:T(8,128)S(1)}, f32[256,512]{1,0:T(8,128)S(1)}, bf16[256,256]{1,0:T(8,128)(2,1)S(1)}) custom-call(s32[4,4]{1,0:T(4,128)} %bitcast.26, bf16[4,256,256]{2,1,0:T(8,128)(2,1)} %bitcast.22, bf16[4,256,512]{2,1,0:T(8,128)(2,1)} %bitcast.21, ...), custom_call_target="tpu_custom_call" | custom-call | flops 1342177280 | bytes 6000000 | tf_op jit(solution)/shard_map/leaf/pallas_call | solution.py:89
  14.3 0.0 collective-permute-done.1.m1r_ref
  14.3 0.0 copy-done.1
  14.3 0.0 copy-start
  14.4 1.3 %first.1 = (f32[256,512]{1,0:T(8,128)S(1)}, f32[256,512]{1,0:T(8,128)S(1)}, f32[256,512]{1,0:T(8,128)S(1)}, bf16[256,256]{1,0:T(8,128)(2,1)S(1)}) custom-call(bf16[256,512]{1,0:T(8,128)(2,1)S(1)} %get-tuple-element.21.t1_ref, f32[256,512]{1,0:T(8,128)S(1)} %get-tuple-element.23.t2_ref, ...), custom_call_target="tpu_custom_call", output_to_operand_aliasing={{0}: (1, {}), {1}: (2, {}), {2}: (3, {})} | custom-call | flops 5000000000 | bytes 3000000 | tf_op jit(solution)/shard_map/first/pallas_call | solution.py:125
  15.6 0.6 all-to-all-done.m2_ref
  16.2 0.0 copy-done
  16.2 2.1 %second.1 = (bf16[8,512,128]{2,1,0:T(8,128)(2,1)}, bf16[256,256]{1,0:T(8,128)(2,1)S(1)}) custom-call(f32[256,512]{1,0:T(8,128)S(1)} %get-tuple-element.26.t2_ref, f32[256,512]{1,0:T(8,128)S(1)} %get-tuple-element.27.t3_ref, f32[256,512]{1,0:T(8,128)S(1)} %get-tuple-element.28.o_ref, bf16[4,3,64,256]{3,2,1,0:T(8,128)(2,1)S(1)} %all-to-all-done.m2_ref, ...), custom_call_target="tpu_custom_call" | custom-call | flops 200000000 | bytes 3000000 | tf_op jit(solution)/shard_map/second/pallas_call | solution.py:158
  18.3 4.7 %all-to-all-start.1 = ((bf16[8,512,128]{2,1,0:T(8,128)(2,1)}), bf16[8,512,128]{2,1,0:T(8,128)(2,1)S(1)}, u32[]{:S(2)}, u32[]{:S(2)}) async-start(bf16[8,512,128]{2,1,0:T(8,128)(2,1)} %get-tuple-element.29), calls=%async_computation.1 | async-start | bytes 2097152 | tf_op jit(solution)/shard_map/all_to_all | solution.py:272
  23.1 3.4 %collective-permute-start = (bf16[256,256]{1,0:T(8,128)(2,1)S(1)}, bf16[256,256]{1,0:T(8,128)(2,1)S(1)}, u32[]{:S(2)}, u32[]{:S(2)}) collective-permute-start(bf16[256,256]{1,0:T(8,128)(2,1)S(1)} %get-tuple-element.22), channel_id=1, source_target_pairs={{0,16},{16,0},{32,48},{48,32},{64,80},{80,64},{96,112},{112,96},{1... | collective-permute-start | bytes 393224 | tf_op jit(solution)/shard_map/ppermute | solution.py:256
  26.4 6.2 %all-to-all-done.1.r8_ref = bf16[8,512,128]{2,1,0:T(8,128)(2,1)S(1)} async-done(((bf16[8,512,128]{2,1,0:T(8,128)(2,1)}), bf16[8,512,128]{2,1,0:T(8,128)(2,1)S(1)}, u32[]{:S(2)}, u32[]{:S(2)}) %all-to-all-start.1) | async-done | bytes 1048608 | tf_op jit(solution)/shard_map/all_to_all | solution.py:272
  32.6 1.2 %third.1 = (bf16[64,256]{1,0:T(8,128)(2,1)}, bf16[16,8,128]{2,1,0:T(8,128)(2,1)}, f32[128,128]{1,0:T(8,128)S(1)}, bf16[128,128]{1,0:T(8,128)(2,1)S(1)}) custom-call(bf16[8,512,128]{2,1,0:T(8,128)(2,1)S(1)} %all-to-all-done.1.r8_ref), custom_call_target="tpu_custom_call" | custom-call | flops 70000000 | bytes 1300000 | tf_op jit(solution)/shard_map/third/pallas_call | solution.py:199
  33.9 16.5 %all-to-all-start.2 = ((bf16[16,8,128]{2,1,0:T(8,128)(2,1)}), bf16[16,8,128]{2,1,0:T(8,128)(2,1)S(1)}, u32[]{:S(2)}, u32[]{:S(2)}) async-start(bf16[16,8,128]{2,1,0:T(8,128)(2,1)} %get-tuple-element.37), calls=%async_computation.2 | async-start | bytes 65536 | tf_op jit(solution)/shard_map/all_to_all | solution.py:274
  50.4 3.1 %collective-permute-start.2 = (bf16[128,128]{1,0:T(8,128)(2,1)S(1)}, bf16[128,128]{1,0:T(8,128)(2,1)S(1)}, u32[]{:S(2)}, u32[]{:S(2)}) collective-permute-start(bf16[128,128]{1,0:T(8,128)(2,1)S(1)} %get-tuple-element.31), channel_id=1, source_target_pairs={{0,64},{16,80},{32,96},{48,112},{64,0},{80,16},{96,32},{112,48},{1... | collective-permute-start | bytes 98312 | tf_op jit(solution)/shard_map/ppermute | solution.py:256
  53.5 0.0 collective-permute-done.came1_ref
  53.5 1.8 %collective-permute-done.2.came2_ref = bf16[128,128]{1,0:T(8,128)(2,1)S(1)} collective-permute-done((bf16[128,128]{1,0:T(8,128)(2,1)S(1)}, bf16[128,128]{1,0:T(8,128)(2,1)S(1)}, u32[]{:S(2)}, u32[]{:S(2)}) %collective-permute-start.2) | collective-permute-done | bytes 32800 | tf_op jit(solution)/shard_map/ppermute | solution.py:256
  55.4 1.1 %lower.1 = (bf16[256,256]{1,0:T(8,128)(2,1)}, bf16[256,128]{1,0:T(8,128)(2,1)}) custom-call(bf16[256,512]{1,0:T(8,128)(2,1)S(1)} %get-tuple-element.21.t1_ref, bf16[256,256]{1,0:T(8,128)(2,1)S(1)} %collective-permute-done.came1_ref, f32[128,128]{1,0:T(8,128)S(1)} %get-tuple-element.30.own2_ref, bf16[128,128]{1,0:T(8,128)(2,1)S(1)} %collective-permute-done.2.came2_ref, ...), custom_call_target="tpu_custom_call" | custom-call | flops 1 | bytes 1 | tf_op jit(solution)/shard_map/lower/pallas_call | solution.py:227
  56.5 1.3 %all-to-all-done.2.r_ref = bf16[16,8,128]{2,1,0:T(8,128)(2,1)S(1)} async-done(((bf16[16,8,128]{2,1,0:T(8,128)(2,1)}), bf16[16,8,128]{2,1,0:T(8,128)(2,1)S(1)}, u32[]{:S(2)}, u32[]{:S(2)}) %all-to-all-start.2) | async-done | bytes 32800 | tf_op jit(solution)/shard_map/all_to_all | solution.py:274
  57.8 0.7 %final.1 = f32[16,64]{1,0:T(8,128)} custom-call(bf16[16,8,128]{2,1,0:T(8,128)(2,1)S(1)} %all-to-all-done.2.r_ref, bf16[256,128]{1,0:T(8,128)(2,1)} %get-tuple-element.35.after_ref), custom_call_target="tpu_custom_call" | custom-call | flops 20000 | bytes 40000 | tf_op jit(solution)/shard_map/final/pallas_call | solution.py:245
Async XLA Ops:
  0.6 13.7 %collective-permute-start.1 = (bf16[128,4,256]{2,1,0:T(4,128)(2,1)}, bf16[128,4,256]{2,1,0:T(4,128)(2,1)S(1)}, u32[]{:S(2)}, u32[]{:S(2)}) collective-permute-start(bf16[128,4,256]{2,1,0:T(4,128)(2,1)} %bitcast.16), channel_id=1, source_target_pairs={{0,16},{16,0},{32,48},{48,32},{64,80},{80,64},{96,112},{112,96},{1... | collective-permute-start | bytes 786440 | tf_op jit(solution)/shard_map/ppermute | solution.py:256
  6.3 10.0 %all-to-all-start = ((bf16[4,3,64,256]{3,2,1,0:T(8,128)(2,1)}), bf16[4,3,64,256]{3,2,1,0:T(8,128)(2,1)S(1)}, u32[]{:S(2)}, u32[]{:S(2)}) async-start(bf16[4,3,64,256]{3,2,1,0:T(8,128)(2,1)} %broadcast_in_dim.12), calls=%async_computation | async-start | bytes 786432 | tf_op jit(solution)/shard_map/all_to_all | solution.py:265
  10.0 4.4 %copy-start.1 = (bf16[128,1,4,256]{3,2,1,0:T(4,128)(2,1)S(1)}, bf16[128,1,4,256]{3,2,1,0:T(4,128)(2,1)}, u32[]{:S(2)}) copy-start(bf16[128,1,4,256]{3,2,1,0:T(4,128)(2,1)} %param.13) | copy-start | bytes 786436
  14.3 1.9 %copy-start = (bf16[32,1,2,256]{3,2,1,0:T(2,128)(2,1)S(1)}, bf16[32,1,2,256]{3,2,1,0:T(2,128)(2,1)}, u32[]{:S(2)}) copy-start(bf16[32,1,2,256]{3,2,1,0:T(2,128)(2,1)} %param.15) | copy-start | bytes 98308
  18.3 14.3 %all-to-all-start.1 = ((bf16[8,512,128]{2,1,0:T(8,128)(2,1)}), bf16[8,512,128]{2,1,0:T(8,128)(2,1)S(1)}, u32[]{:S(2)}, u32[]{:S(2)}) async-start(bf16[8,512,128]{2,1,0:T(8,128)(2,1)} %get-tuple-element.29), calls=%async_computation.1 | async-start | bytes 2097152 | tf_op jit(solution)/shard_map/all_to_all | solution.py:272
  23.1 30.4 %collective-permute-start = (bf16[256,256]{1,0:T(8,128)(2,1)S(1)}, bf16[256,256]{1,0:T(8,128)(2,1)S(1)}, u32[]{:S(2)}, u32[]{:S(2)}) collective-permute-start(bf16[256,256]{1,0:T(8,128)(2,1)S(1)} %get-tuple-element.22), channel_id=1, source_target_pairs={{0,16},{16,0},{32,48},{48,32},{64,80},{80,64},{96,112},{112,96},{1... | collective-permute-start | bytes 393224 | tf_op jit(solution)/shard_map/ppermute | solution.py:256
  33.9 23.9 %all-to-all-start.2 = ((bf16[16,8,128]{2,1,0:T(8,128)(2,1)}), bf16[16,8,128]{2,1,0:T(8,128)(2,1)S(1)}, u32[]{:S(2)}, u32[]{:S(2)}) async-start(bf16[16,8,128]{2,1,0:T(8,128)(2,1)} %get-tuple-element.37), calls=%async_computation.2 | async-start | bytes 65536 | tf_op jit(solution)/shard_map/all_to_all | solution.py:274
  50.4 5.0 %collective-permute-start.2 = (bf16[128,128]{1,0:T(8,128)(2,1)S(1)}, bf16[128,128]{1,0:T(8,128)(2,1)S(1)}, u32[]{:S(2)}, u32[]{:S(2)}) collective-permute-start(bf16[128,128]{1,0:T(8,128)(2,1)S(1)} %get-tuple-element.31), channel_id=1, source_target_pairs={{0,64},{16,80},{32,96},{48,112},{64,0},{80,16},{96,32},{112,48},{1... | collective-permute-start | bytes 98312 | tf_op jit(solution)/shard_map/ppermute | solution.py:256

commit v2 on v1

v2 whole, which is shorter than its diff:
```python
import jax
import jax.numpy as jnp
from jax import lax
from jax.experimental import pallas as pl
from jax.experimental.pallas import tpu as pltpu
from jax.sharding import PartitionSpec as P

F32 = jnp.float32
BF16 = jnp.bfloat16
LEAF_BYTES = 12 << 20
TRANSFORM_BYTES = 6 << 20
SMALL_BYTES = 4 << 20
GROUPS_8 = [[g * 8 + i for i in range(8)] for g in range(4)]
GROUPS_4 = [[g * 4 + i for i in range(4)] for g in range(8)]


def in_vmem(x):
    return pltpu.with_memory_space_constraint(x, pltpu.VMEM)


def in_hbm(x):
    return pltpu.with_memory_space_constraint(x, pltpu.HBM)


def dot(a, b):
    return jnp.dot(a, b, preferred_element_type=F32)


def dot_wide(a, b):
    high = b.astype(BF16)
    low = (b - high.astype(F32)).astype(BF16)
    return dot(a, high) + dot(a, low)


def low_lanes(shape):
    return lax.broadcasted_iota(jnp.int32, shape, 1) < 64


def join_halves(first, second, upper):
    low = low_lanes(first.shape)
    if upper:
        return jnp.where(low, pltpu.roll(first, 64, 1), second)
    return jnp.where(low, first, pltpu.roll(second, 64, 1))


def tile(ref, t):
    return ref[:, t * 128 : (t + 1) * 128]


def spread_kernel(x_ref, out_hbm, sems):
    copies = [pltpu.make_async_copy(x_ref, out_hbm.at[i], sems.at[i]) for i in range(4)]
    for copy in copies:
        copy.start()
    for copy in copies:
        copy.wait()


def spread(x):
    return pl.pallas_call(
        spread_kernel,
        name="spread",
        in_specs=[pl.BlockSpec(memory_space=pltpu.VMEM)],
        out_specs=pl.BlockSpec(memory_space=pl.ANY),
        out_shape=pltpu.HBM((4,) + x.shape, x.dtype),
        scratch_shapes=[pltpu.SemaphoreType.DMA((4,))],
        compiler_params=pltpu.CompilerParams(vmem_limit_bytes=1 << 20),
        cost_estimate=pl.CostEstimate(flops=1000, bytes_accessed=500_000, transcendentals=0),
    )(in_vmem(x))


def leaf_kernel(
    w_ref, inv_hbm, rhs_hbm, blk_hbm, out_hbm, m3_hbm,
    t1_ref, t2_ref, t3_ref, o_ref, sent_ref, a8_hbm,
    inv, rhs, blk, out, y, masked, m3, folded, sems, sends,
):
    copies = []
    for j in range(4):
        pairs = ((inv_hbm, inv), (rhs_hbm, rhs), (blk_hbm, blk), (out_hbm, out))
        copies.append([pltpu.make_async_copy(a.at[j], b.at[j], sems.at[j, i]) for i, (a, b) in enumerate(pairs)])
    third = pltpu.make_async_copy(m3_hbm, m3, sems.at[0, 4])
    third.start()
    for first in (0, 2):
        for j in range(4):
            for copy in copies[j][first : first + 2]:
                copy.start()
    third.wait()
    for slot in range(2):
        for side in range(2):
            start = side * 64 + slot * 32
            folded[start : start + 32] = m3[:, slot, side * 128 : (side + 1) * 128]
    blocks = [pltpu.make_async_copy(folded, a8_hbm.at[k, 256:384], sends.at[k]) for k in range(8)]
    for copy in blocks:
        copy.start()
    for j in range(4):
        copies[j][0].wait()
        copies[j][1].wait()
        y[j * 256 : (j + 1) * 256, :] = dot(inv[j], rhs[j]).astype(BF16)
    for j in range(4):
        copies[j][2].wait()
        copies[j][3].wait()
        for t in range(4):
            block = blk[j, t] if t < 3 else out[j]
            masked[t, :, j * 256 : (j + 1) * 256] = block * w_ref[j, t].astype(F32).astype(BF16)
    for t, into in enumerate((t1_ref, t2_ref, t3_ref, o_ref)):
        into[...] = dot(masked[t], y[...]).astype(into.dtype)
    for half in range(2):
        sent_ref[:, half * 128 : (half + 1) * 128] = own_and_other(t1_ref, half)[1].astype(BF16)
    for copy in blocks:
        copy.wait()


def own_and_other(t1_ref, half):
    first, second = tile(t1_ref, 2 * half).astype(F32), tile(t1_ref, 2 * half + 1).astype(F32)
    even = join_halves(first, second, False)
    odd = join_halves(first, second, True)
    own_upper = (lax.axis_index("srow") & 1) == 1
    return jnp.where(own_upper, odd, even), jnp.where(own_upper, even, odd)


def leaf_terms(weights, inverse, rhs, blocks, outer, m3):
    full = pltpu.VMEM((256, 512), F32)
    return pl.pallas_call(
        leaf_kernel,
        name="leaf",
        in_specs=[pl.BlockSpec(memory_space=pltpu.SMEM)] + [pl.BlockSpec(memory_space=pl.ANY)] * 5,
        out_specs=[pl.BlockSpec(memory_space=pltpu.VMEM)] * 5 + [pl.BlockSpec(memory_space=pl.ANY)],
        out_shape=[
            pltpu.VMEM((256, 512), BF16), full, full, full, pltpu.VMEM((256, 256), BF16),
            pltpu.HBM((8, 384, 128), BF16),
        ],
        scratch_shapes=[
            pltpu.VMEM((4, 256, 256), BF16),
            pltpu.VMEM((4, 256, 512), BF16),
            pltpu.VMEM((4, 3, 256, 256), BF16),
            pltpu.VMEM((4, 256, 256), BF16),
            pltpu.VMEM((1024, 512), BF16),
            pltpu.VMEM((4, 256, 1024), BF16),
            pltpu.VMEM((32, 2, 256), BF16),
            pltpu.VMEM((128, 128), BF16),
            pltpu.SemaphoreType.DMA((4, 5)),
            pltpu.SemaphoreType.DMA((8,)),
        ],
        compiler_params=pltpu.CompilerParams(vmem_limit_bytes=LEAF_BYTES),
        cost_estimate=pl.CostEstimate(flops=1_342_177_280, bytes_accessed=6_000_000, transcendentals=0),
    )(*map(in_hbm, (weights, inverse, rhs, blocks, outer, m3)))


def first_kernel(t1_ref, t2_ref, t3_ref, o_ref, m1_ref, m1r_ref, t2n_ref, t3n_ref, on_ref, d1_ref, sent_ref, kept_ref, one, shares):
    row = lax.axis_index("srow")
    own = pl.multiple_of((row & 1) * 128, 128)
    other = pl.multiple_of(128 - (row & 1) * 128, 128)
    for slot in range(4):
        into = d1_ref if slot == 0 else one.at[slot - 1]
        into[pl.ds(own, 128), :] = m1_ref[:, slot, :]
        into[pl.ds(other, 128), :] = m1r_ref[:, slot, :]
    x1 = dot(d1_ref[...], t1_ref[...]).astype(BF16)
    under = dot(one[...].reshape(768, 256), x1)
    t2 = t2_ref[...] - under[:256]
    t2n_ref[...] = t2
    for t in range(2):
        first, second = t2[:, t * 128 : (t + 1) * 128], t2[:, (t + 2) * 128 : (t + 3) * 128]
        shares[2 * t] = join_halves(first, second, False)
        shares[2 * t + 1] = join_halves(first, second, True)
    place = row & 3
    for i in range(2):
        kept_ref[i] = shares[place ^ i].astype(BF16)
        sent_ref[i] = shares[place ^ 3 ^ i].astype(BF16)
    t3n_ref[...] = t3_ref[...] - under[256:512]
    on_ref[...] = o_ref[...] - under[512:]


def first_level(t1, t2, t3, o, m1, m1r):
    full = pltpu.VMEM((256, 512), F32)
    two = pltpu.VMEM((2, 256, 128), BF16)
    return pl.pallas_call(
        first_kernel,
        name="first",
        out_shape=[full, full, full, pltpu.VMEM((256, 256), BF16), two, two],
        scratch_shapes=[pltpu.VMEM((3, 256, 256), BF16), pltpu.VMEM((4, 256, 128), F32)],
        input_output_aliases={1: 0, 2: 1, 3: 2},
        compiler_params=pltpu.CompilerParams(vmem_limit_bytes=TRANSFORM_BYTES),
        cost_estimate=pl.CostEstimate(flops=5_000_000_000, bytes_accessed=3_000_000, transcendentals=0),
    )(*map(in_vmem, (t1, t2, t3, o, m1, m1r)))


def second_kernel(t2_ref, t3_ref, o_ref, m2_ref, blocks_ref, a8_hbm, d2_ref, two, a8, sems):
    for q in range(4):
        for slot in range(3):
            into = d2_ref if slot == 0 else two.at[slot - 1]
            into[q * 64 : (q + 1) * 64, :] = m2_ref[q, slot]
    x2 = dot(d2_ref[...], t2_ref[...].astype(BF16)).astype(BF16)
    copies = []
    for half in range(2):
        wide = slice(half * 256, half * 256 + 256)
        above = dot(two[...].reshape(512, 256), x2[:, wide])
        t3 = t3_ref[:, wide] - above[:256]
        o = o_ref[:, wide] - above[256:]
        for i in range(4):
            k = half * 4 + i
            cut = slice(i // 2 * 128, i // 2 * 128 + 128)
            a8[k] = join_halves(t3[:, cut], o[:, cut], i % 2 == 1).astype(BF16)
            copies.append(pltpu.make_async_copy(a8.at[k], a8_hbm.at[k, :256], sems.at[k]))
            copies[-1].start()
    for copy in copies:
        copy.wait()


def second_level(t2, t3, o, m2, blocks):
    return pl.pallas_call(
        second_kernel,
        name="second",
        in_specs=[pl.BlockSpec(memory_space=pltpu.VMEM)] * 4 + [pl.BlockSpec(memory_space=pl.ANY)],
        out_specs=[pl.BlockSpec(memory_space=pl.ANY), pl.BlockSpec(memory_space=pltpu.VMEM)],
        out_shape=[pltpu.HBM((8, 384, 128), BF16), pltpu.VMEM((256, 256), BF16)],
        scratch_shapes=[
            pltpu.VMEM((2, 256, 256), BF16),
            pltpu.VMEM((8, 256, 128), BF16),
            pltpu.SemaphoreType.DMA((8,)),
        ],
        input_output_aliases={4: 0},
        compiler_params=pltpu.CompilerParams(vmem_limit_bytes=TRANSFORM_BYTES),
        cost_estimate=pl.CostEstimate(flops=200_000_000, bytes_accessed=3_000_000, transcendentals=0),
    )(*map(in_vmem, (t2, t3, o, m2)), in_hbm(blocks))


def third_kernel(r8_ref, x3_ref, out_ref, d3, l3, v):
    total = r8_ref[0, :256].astype(F32)
    for k in range(1, 8):
        total = total + r8_ref[k, :256].astype(F32)
    for k in range(8):
        for side in range(2):
            cut = slice(side * 128, (side + 1) * 128)
            start = 256 + side * 64
            d3[k * 32 : (k + 1) * 32, cut] = r8_ref[k, start : start + 32]
            l3[k * 32 : (k + 1) * 32, cut] = r8_ref[k, start + 32 : start + 64]
    x3 = -dot_wide(d3[...], total)
    x3_ref[...] = jnp.transpose(x3)[:64, :].astype(BF16)
    v[...] = total + pltpu.roll(dot_wide(l3[...], x3), 64, 1)
    low = low_lanes((8, 128))
    for p in range(16):
        upper, lower = v[p * 16 : p * 16 + 8, :], v[p * 16 + 8 : p * 16 + 16, :]
        out_ref[p] = jnp.where(low, pltpu.roll(upper, 64, 1), lower)


def middle_kernel(kept_ref, came_ref, own_ref, sent_ref):
    own_ref[...] = kept_ref[0].astype(F32) + came_ref[0].astype(F32)
    sent_ref[...] = (kept_ref[1].astype(F32) + came_ref[1].astype(F32)).astype(BF16)


def middle_sums(kept, came):
    return pl.pallas_call(
        middle_kernel,
        name="middle",
        out_shape=[pltpu.VMEM((256, 128), F32), pltpu.VMEM((256, 128), BF16)],
        compiler_params=pltpu.CompilerParams(vmem_limit_bytes=SMALL_BYTES),
        cost_estimate=pl.CostEstimate(flops=1, bytes_accessed=1, transcendentals=0),
    )(in_vmem(kept), in_vmem(came))


def third_level(r8):
    return pl.pallas_call(
        third_kernel,
        name="third",
        out_shape=[
            jax.ShapeDtypeStruct((64, 256), BF16),
            pltpu.VMEM((16, 8, 128), F32),
        ],
        scratch_shapes=[pltpu.VMEM((256, 256), BF16), pltpu.VMEM((256, 256), BF16), pltpu.VMEM((256, 128), F32)],
        compiler_params=pltpu.CompilerParams(vmem_limit_bytes=SMALL_BYTES),
        cost_estimate=pl.CostEstimate(flops=70_000_000, bytes_accessed=1_300_000, transcendentals=0),
    )(in_vmem(r8))


def lower_kernel(t1_ref, came1_ref, own2_ref, came2_ref, d1_ref, d2_ref, x1_ref, x2_ref):
    kept_one = jnp.concatenate([own_and_other(t1_ref, half)[0] for half in range(2)], axis=1)
    sum_one = kept_one + came1_ref[...].astype(F32)
    x1_ref[...] = (-dot_wide(d1_ref[...], sum_one)).astype(BF16)
    x2_ref[...] = (-dot_wide(d2_ref[...], own2_ref[...] + came2_ref[...].astype(F32))).astype(BF16)


def lower_levels(t1, came1, own2, came2, d1, d2):
    return pl.pallas_call(
        lower_kernel,
        name="lower",
        out_shape=[jax.ShapeDtypeStruct((256, 256), BF16), jax.ShapeDtypeStruct((256, 128), BF16)],
        compiler_params=pltpu.CompilerParams(vmem_limit_bytes=SMALL_BYTES),
        cost_estimate=pl.CostEstimate(flops=1, bytes_accessed=1, transcendentals=0),
    )(*map(in_vmem, (t1, came1, own2, came2, d1, d2)))


def final_kernel(r_ref, after_ref, out_ref):
    total = r_ref[0]
    for k in range(1, 16):
        total = total + r_ref[k]
    out_ref[0:8, :] = total[:, :64]
    out_ref[8:16, :] = pltpu.roll(total, 64, 1)[:, :64]


def final_sum(received, after):
    return pl.pallas_call(
        final_kernel,
        name="final",
        in_specs=[pl.BlockSpec(memory_space=pltpu.VMEM), pl.BlockSpec(memory_space=pl.ANY)],
        out_shape=jax.ShapeDtypeStruct((16, 64), F32),
        compiler_params=pltpu.CompilerParams(vmem_limit_bytes=SMALL_BYTES),
        cost_estimate=pl.CostEstimate(flops=20_000, bytes_accessed=40_000, transcendentals=0),
    )(in_vmem(received), in_hbm(after))


def swap(block, flip):
    return lax.ppermute(block, "srow", [(i, i ^ flip) for i in range(32)])


def shards(
    leaf_rhs, leaf_inverse, leaf_blocks, leaf_outer, leaf_targets, level_one, level_two, level_three
):
    m1, m3 = level_one[:, 0], level_three[:, 0]
    m1r = swap(m1, 1)
    m2 = spread(jnp.transpose(level_two[:, 0], (1, 0, 2)))
    m2 = lax.all_to_all(m2, "srow", 0, 0, axis_index_groups=GROUPS_4, tiled=True)
    t1, t2, t3, o, sent1, a8 = leaf_terms(
        leaf_targets[0, 0], leaf_inverse[0, 0], leaf_rhs[0, 0], leaf_blocks[0, 0], leaf_outer[0, 0], m3
    )
    came1 = swap(sent1, 1)
    t2, t3, o, d1, sent2, kept2 = first_level(t1, t2, t3, o, m1, m1r)
    a8, d2 = second_level(t2, t3, o, m2, a8)
    r8 = lax.all_to_all(a8, "srow", 0, 0, axis_index_groups=GROUPS_8, tiled=True)
    x3, parts = third_level(r8)
    own2, sent2 = middle_sums(kept2, swap(sent2, 3))
    received = lax.all_to_all(parts, "scol", 0, 0, tiled=True)
    x1, x2 = lower_levels(t1, came1, own2, swap(sent2, 1), d1, d2)
    outer_update = final_sum(received, x2)
    return (x1[:, None, :], x2[:, None, :], jnp.transpose(x3)[:, None, :], outer_update)


def solution(mesh):
    placed = (
        P("srow", "scol", None, None, None),
        P("srow", "scol", None, None, None),
        P("srow", "scol", None, None, None, None),
        P("srow", "scol", None, None, None),
        P("srow", "scol", None, None),
        P("srow", "scol", None, None),
        P("srow", "scol", None, None),
        P("srow", "scol", None, None),
    )
    return jax.shard_map(
        shards,
        mesh=mesh,
        in_specs=placed,
        out_specs=(
            P(None, "scol", "srow"),
            P(None, "scol", "srow"),
            P(None, "scol", "srow"),
            P("scol", "srow"),
        ),
        check_vma=False,
    )
```

time: 58.9 us -> 57.4 us (0.975)
  waiting for transfers between devices: 9.92 us -> 6.6 us
  starting transfers between devices: 35.4 us -> 37.6 us
  local copies, waits for them, and re-layouts: 1.68 us -> 0.89 us
    all_to_all x1, waiting for transfers between devices: 6.22 us -> 1.88 us  [shards(): lax.all_to_all(a8, 'srow', 0, 0, axis_index_groups=GROUPS_8, tiled=True)]
    ppermute x3 -> x4, starting transfers between devices: 10.4 us -> 12.7 us  [swap(): return lax.ppermute(block, 'srow', [(i, i ^ flip) for i in range(32)])]
    broadcast_in_dim x1 -> x0, local copies, waits for them, and re-layouts: 1.67 us -> none  [shards(): jnp.broadcast_to(jnp.transpose(level_two[:, 0], (1, 0, 2)), (4, 3, 64, 256))]
    ppermute x3 -> x4, waiting for transfers between devices: 1.84 us -> 3.24 us  [swap(): return lax.ppermute(block, 'srow', [(i, i ^ flip) for i in range(32)])]
    unnamed x4, local copies, waits for them, and re-layouts: 0.01 us -> 0.89 us
    pallas_call x2 -> x4, Pallas kernels: 3.36 us -> 3.52 us  [the longest x1 1.44 us: second_level(): pl.pallas_call(second_kernel, name='second', in_specs=[pl.BlockSpec(memor...]
  transfers between devices with their start and end apart: 6 -> 7, of which waited for: 4 -> 4; matrix products, arithmetic and copies ran while one was open for 3% -> 0% of each run, Pallas kernels for 14% -> 16%
where the time goes in v2:
time: 57.4 us; the launch traced here: 56.9 us
  starting transfers between devices  37.6 us (66%)
  Pallas kernels  11.1 us (19%)
  waiting for transfers between devices  6.6 us (11%)
  local copies, waits for them, and re-layouts  0.89 us (2%)
  between operations  0.74 us (1%)
    all_to_all x1, starting transfers between devices, shards(): received = lax.all_to_all(parts, 'scol', 0, 0, tiled=True)  16.2 us
    ppermute x4, starting transfers between devices, swap(): return lax.ppermute(block, 'srow', [(i, i ^ flip) for i in range(32)])  12.7 us
    all_to_all x1, starting transfers between devices, shards(): lax.all_to_all(a8, 'srow', 0, 0, axis_index_groups=GROUPS_8, tiled=True)  4.92 us
    pallas_call x1, Pallas kernels, leaf_terms(): pl.pallas_call(leaf_kernel, name='leaf', in_specs=[pl.BlockSpec(memory_sp...  4.49 us
    all_to_all x1, starting transfers between devices, shards(): lax.all_to_all(m2, 'srow', 0, 0, axis_index_groups=GROUPS_4, tiled=True)  3.73 us
    ppermute x4, waiting for transfers between devices, swap(): return lax.ppermute(block, 'srow', [(i, i ^ flip) for i in range(32)])  3.24 us
    all_to_all x1, waiting for transfers between devices, shards(): lax.all_to_all(a8, 'srow', 0, 0, axis_index_groups=GROUPS_8, tiled=True)  1.88 us
    pallas_call x1, Pallas kernels, second_level(): pl.pallas_call(second_kernel, name='second', in_specs=[pl.BlockSpec(memor...  1.44 us
  transfers between devices with their start and end apart: 7, of which 4 were waited for; matrix products, arithmetic and copies ran while one was open for 0% of the time, Pallas kernels for 16%

profile of v2, /device:TPU:1, one launch (start us, length us, event | category | flops | bytes accessed | tf_op | source)
XLA Modules:
  0.0 56.9 jit_solution(9453000402134359111)
XLA Ops:
  0.6 4.0 %collective-permute-start.1 = (bf16[128,4,256]{2,1,0:T(4,128)(2,1)}, bf16[128,4,256]{2,1,0:T(4,128)(2,1)S(1)}, u32[]{:S(2)}, u32[]{:S(2)}) collective-permute-start(bf16[128,4,256]{2,1,0:T(4,128)(2,1)} %bitcast.16), channel_id=1, source_target_pairs={{0,16},{16,0},{32,48},{48,32},{64,80},{80,64},{96,112},{112,96},{1... | collective-permute-start | bytes 786440 | tf_op jit(solution)/shard_map/ppermute | solution.py:311
  4.6 0.0 copy-start
  4.6 0.9 %copy-done = bf16[64,1,3,256]{3,0,2,1:T(8,128)(2,1)S(1)} copy-done((bf16[64,1,3,256]{3,0,2,1:T(8,128)(2,1)S(1)}, bf16[64,1,3,256]{3,0,2,1:T(8,128)(2,1)}, u32[]{:S(2)}) %copy-start) | copy-done | bytes 98328
  5.5 0.8 %spread.1 = bf16[4,3,64,256]{3,2,1,0:T(8,128)(2,1)} custom-call(bf16[3,64,256]{2,1,0:T(8,128)(2,1)S(1)} %bitcast.15), custom_call_target="tpu_custom_call" | custom-call | flops 1000 | bytes 500000 | tf_op jit(solution)/shard_map/spread/pallas_call | solution.py:59
  6.3 3.7 %all-to-all-start = ((bf16[4,3,64,256]{3,2,1,0:T(8,128)(2,1)}), bf16[4,3,64,256]{3,2,1,0:T(8,128)(2,1)S(1)}, u32[]{:S(2)}, u32[]{:S(2)}) async-start(bf16[4,3,64,256]{3,2,1,0:T(8,128)(2,1)} %spread.1), calls=%async_computation | async-start | bytes 786432 | tf_op jit(solution)/shard_map/all_to_all | solution.py:320
  10.0 0.0 copy-start.1
  10.0 4.5 %leaf.1 = (bf16[256,512]{1,0:T(8,128)(2,1)S(1)}, f32[256,512]{1,0:T(8,128)S(1)}, f32[256,512]{1,0:T(8,128)S(1)}, f32[256,512]{1,0:T(8,128)S(1)}, bf16[256,256]{1...) custom-call(s32[4,4]{1,0:T(4,128)} %bitcast.26, bf16[4,256,256]{2,1,0:T(8,128)(2,1)} %bitcast.21, ...), custom_call_target="tpu_custom_call" | custom-call | flops 1342177280 | bytes 6000000 | tf_op jit(solution)/shard_map/leaf/pallas_call | solution.py:122
  14.5 0.0 collective-permute-done.1.m1r_ref
  14.5 0.0 copy-done.1
  14.5 1.3 %first.1 = (f32[256,512]{1,0:T(8,128)S(1)}, f32[256,512]{1,0:T(8,128)S(1)}, f32[256,512]{1,0:T(8,128)S(1)}, bf16[256,256]{1,0:T(8,128)(2,1)S(1)}, bf16[2,256,128...) custom-call(bf16[256,512]{1,0:T(8,128)(2,1)S(1)} %get-tuple-element., ...), custom_call_target="tpu_custom_call", output_to_operand_aliasing={{0}: (1, {}), {1}: (2, {}), {2}: (3, {})} | custom-call | flops 5000000000 | bytes 3000000 | tf_op jit(solution)/shard_map/first/pallas_call | solution.py:175
  15.9 0.4 all-to-all-done.m2_ref
  16.2 1.4 %second.1 = (bf16[8,384,128]{2,1,0:T(8,128)(2,1)}, bf16[256,256]{1,0:T(8,128)(2,1)S(1)}) custom-call(f32[256,512]{1,0:T(8,128)S(1)} %get-tuple-element.34.t2_ref, f32[256,512]{1,0:T(8,128)S(1)} %get-tuple-element.35.t3_ref, f32[256,512]{1,0:T(8,128)S(1)} %get-tuple-element.36.o_ref, ...), custom_call_target="tpu_custom_call", output_to_operand_aliasing={{0}: (4, {})} | custom-call | flops 200000000 | bytes 3000000 | tf_op jit(solution)/shard_map/second/pallas_call | solution.py:209
  17.7 4.9 %all-to-all-start.1 = ((bf16[8,384,128]{2,1,0:T(8,128)(2,1)}), bf16[8,384,128]{2,1,0:T(8,128)(2,1)S(1)}, u32[]{:S(2)}, u32[]{:S(2)}) async-start(bf16[8,384,128]{2,1,0:T(8,128)(2,1)} %get-tuple-element.41), calls=%async_computation.1 | async-start | bytes 1572864 | tf_op jit(solution)/shard_map/all_to_all | solution.py:327
  22.6 4.6 %collective-permute-start.2 = (bf16[2,256,128]{2,1,0:T(8,128)(2,1)S(1)}, bf16[2,256,128]{2,1,0:T(8,128)(2,1)S(1)}, u32[]{:S(2)}, u32[]{:S(2)}) collective-permute-start(bf16[2,256,128]{2,1,0:T(8,128)(2,1)S(1)} %get-tuple-element.30), channel_id=1, source_target_pairs={{0,48},{16,32},{32,16},{48,0},{64,112},{80,96},{96,80},{112,64},{1... | collective-permute-start | bytes 393224 | tf_op jit(solution)/shard_map/ppermute | solution.py:311
  27.2 1.9 %collective-permute-start = (bf16[256,256]{1,0:T(8,128)(2,1)S(1)}, bf16[256,256]{1,0:T(8,128)(2,1)S(1)}, u32[]{:S(2)}, u32[]{:S(2)}) collective-permute-start(bf16[256,256]{1,0:T(8,128)(2,1)S(1)} %get-tuple-element.25), channel_id=1, source_target_pairs={{0,16},{16,0},{32,48},{48,32},{64,80},{80,64},{96,112},{112,96},{1... | collective-permute-start | bytes 393224 | tf_op jit(solution)/shard_map/ppermute | solution.py:311
  29.1 1.9 %all-to-all-done.1.r8_ref = bf16[8,384,128]{2,1,0:T(8,128)(2,1)S(1)} async-done(((bf16[8,384,128]{2,1,0:T(8,128)(2,1)}), bf16[8,384,128]{2,1,0:T(8,128)(2,1)S(1)}, u32[]{:S(2)}, u32[]{:S(2)}) %all-to-all-start.1) | async-done | bytes 786464 | tf_op jit(solution)/shard_map/all_to_all | solution.py:327
  31.0 1.3 %third.1 = (bf16[64,256]{1,0:T(8,128)(2,1)}, f32[16,8,128]{2,1,0:T(8,128)}) custom-call(bf16[8,384,128]{2,1,0:T(8,128)(2,1)S(1)} %all-to-all-done.1.r8_ref), custom_call_target="tpu_custom_call" | custom-call | flops 70000000 | bytes 1300000 | tf_op jit(solution)/shard_map/third/pallas_call | solution.py:261
  32.3 16.2 %all-to-all-start.2 = ((f32[16,8,128]{2,1,0:T(8,128)}), f32[16,8,128]{2,1,0:T(8,128)S(1)}, u32[]{:S(2)}, u32[]{:S(2)}) async-start(f32[16,8,128]{2,1,0:T(8,128)} %get-tuple-element.43), calls=%async_computation.2 | async-start | bytes 131072 | tf_op jit(solution)/shard_map/all_to_all | solution.py:330
  48.4 0.0 collective-permute-done.2.came_ref
  48.5 2.3 %collective-permute-start.3 = (bf16[256,128]{1,0:T(8,128)(2,1)S(1)}, bf16[256,128]{1,0:T(8,128)(2,1)S(1)}, u32[]{:S(2)}, u32[]{:S(2)}) collective-permute-start(bf16[256,128]{1,0:T(8,128)(2,1)S(1)} %get-tuple-element.32), channel_id=1, source_target_pairs={{0,16},{16,0},{32,48},{48,32},{64,80},{80,64},{96,112},{112,96},{1... | collective-permute-start | bytes 196616 | tf_op jit(solution)/shard_map/ppermute | solution.py:311
  50.8 0.0 collective-permute-done.came1_ref
  50.8 3.2 %collective-permute-done.3.came2_ref = bf16[256,128]{1,0:T(8,128)(2,1)S(1)} collective-permute-done((bf16[256,128]{1,0:T(8,128)(2,1)S(1)}, bf16[256,128]{1,0:T(8,128)(2,1)S(1)}, u32[]{:S(2)}, u32[]{:S(2)}) %collective-permute-start.3) | collective-permute-done | bytes 65568 | tf_op jit(solution)/shard_map/ppermute | solution.py:311
  54.0 1.1 %lower.1 = (bf16[256,256]{1,0:T(8,128)(2,1)}, bf16[256,128]{1,0:T(8,128)(2,1)}) custom-call(bf16[256,512]{1,0:T(8,128)(2,1)S(1)} %get-tuple-element.24.t1_ref, bf16[256,256]{1,0:T(8,128)(2,1)S(1)} %collective-permute-done.came1_ref, f32[256,128]{1,0:T(8,128)S(1)} %get-tuple-element.31.own2_ref, bf16[256,128]{1,0:T(8,128)(2,1)S(1)} %collective-permute-done.3.came2_ref, ...), custom_call_target="tpu_custom_call" | custom-call | flops 1 | bytes 1 | tf_op jit(solution)/shard_map/lower/pallas_call | solution.py:282
  55.1 1.1 %all-to-all-done.2.r_ref = f32[16,8,128]{2,1,0:T(8,128)S(1)} async-done(((f32[16,8,128]{2,1,0:T(8,128)}), f32[16,8,128]{2,1,0:T(8,128)S(1)}, u32[]{:S(2)}, u32[]{:S(2)}) %all-to-all-start.2) | async-done | bytes 65568 | tf_op jit(solution)/shard_map/all_to_all | solution.py:330
  56.2 0.7 %final.1 = f32[16,64]{1,0:T(8,128)} custom-call(f32[16,8,128]{2,1,0:T(8,128)S(1)} %all-to-all-done.2.r_ref, bf16[256,128]{1,0:T(8,128)(2,1)} %get-tuple-element.40.after_ref), custom_call_target="tpu_custom_call" | custom-call | flops 20000 | bytes 40000 | tf_op jit(solution)/shard_map/final/pallas_call | solution.py:300
  (1 shorter events, 0.0 us)
Async XLA Ops:
  0.6 13.9 %collective-permute-start.1 = (bf16[128,4,256]{2,1,0:T(4,128)(2,1)}, bf16[128,4,256]{2,1,0:T(4,128)(2,1)S(1)}, u32[]{:S(2)}, u32[]{:S(2)}) collective-permute-start(bf16[128,4,256]{2,1,0:T(4,128)(2,1)} %bitcast.16), channel_id=1, source_target_pairs={{0,16},{16,0},{32,48},{48,32},{64,80},{80,64},{96,112},{112,96},{1... | collective-permute-start | bytes 786440 | tf_op jit(solution)/shard_map/ppermute | solution.py:311
  4.6 0.9 %copy-start = (bf16[64,1,3,256]{3,0,2,1:T(8,128)(2,1)S(1)}, bf16[64,1,3,256]{3,0,2,1:T(8,128)(2,1)}, u32[]{:S(2)}) copy-start(bf16[64,1,3,256]{3,0,2,1:T(8,128)(2,1)} %param.14) | copy-start | bytes 294916
  6.3 10.0 %all-to-all-start = ((bf16[4,3,64,256]{3,2,1,0:T(8,128)(2,1)}), bf16[4,3,64,256]{3,2,1,0:T(8,128)(2,1)S(1)}, u32[]{:S(2)}, u32[]{:S(2)}) async-start(bf16[4,3,64,256]{3,2,1,0:T(8,128)(2,1)} %spread.1), calls=%async_computation | async-start | bytes 786432 | tf_op jit(solution)/shard_map/all_to_all | solution.py:320
  10.0 4.5 %copy-start.1 = (bf16[128,1,4,256]{3,2,1,0:T(4,128)(2,1)S(1)}, bf16[128,1,4,256]{3,2,1,0:T(4,128)(2,1)}, u32[]{:S(2)}) copy-start(bf16[128,1,4,256]{3,2,1,0:T(4,128)(2,1)} %param.13) | copy-start | bytes 786436
  17.7 13.3 %all-to-all-start.1 = ((bf16[8,384,128]{2,1,0:T(8,128)(2,1)}), bf16[8,384,128]{2,1,0:T(8,128)(2,1)S(1)}, u32[]{:S(2)}, u32[]{:S(2)}) async-start(bf16[8,384,128]{2,1,0:T(8,128)(2,1)} %get-tuple-element.41), calls=%async_computation.1 | async-start | bytes 1572864 | tf_op jit(solution)/shard_map/all_to_all | solution.py:327
  22.6 25.8 %collective-permute-start.2 = (bf16[2,256,128]{2,1,0:T(8,128)(2,1)S(1)}, bf16[2,256,128]{2,1,0:T(8,128)(2,1)S(1)}, u32[]{:S(2)}, u32[]{:S(2)}) collective-permute-start(bf16[2,256,128]{2,1,0:T(8,128)(2,1)S(1)} %get-tuple-element.30), channel_id=1, source_target_pairs={{0,48},{16,32},{32,16},{48,0},{64,112},{80,96},{96,80},{112,64},{1... | collective-permute-start | bytes 393224 | tf_op jit(solution)/shard_map/ppermute | solution.py:311
  27.2 23.6 %collective-permute-start = (bf16[256,256]{1,0:T(8,128)(2,1)S(1)}, bf16[256,256]{1,0:T(8,128)(2,1)S(1)}, u32[]{:S(2)}, u32[]{:S(2)}) collective-permute-start(bf16[256,256]{1,0:T(8,128)(2,1)S(1)} %get-tuple-element.25), channel_id=1, source_target_pairs={{0,16},{16,0},{32,48},{48,32},{64,80},{80,64},{96,112},{112,96},{1... | collective-permute-start | bytes 393224 | tf_op jit(solution)/shard_map/ppermute | solution.py:311
  32.3 24.0 %all-to-all-start.2 = ((f32[16,8,128]{2,1,0:T(8,128)}), f32[16,8,128]{2,1,0:T(8,128)S(1)}, u32[]{:S(2)}, u32[]{:S(2)}) async-start(f32[16,8,128]{2,1,0:T(8,128)} %get-tuple-element.43), calls=%async_computation.2 | async-start | bytes 131072 | tf_op jit(solution)/shard_map/all_to_all | solution.py:330
  48.5 5.6 %collective-permute-start.3 = (bf16[256,128]{1,0:T(8,128)(2,1)S(1)}, bf16[256,128]{1,0:T(8,128)(2,1)S(1)}, u32[]{:S(2)}, u32[]{:S(2)}) collective-permute-start(bf16[256,128]{1,0:T(8,128)(2,1)S(1)} %get-tuple-element.32), channel_id=1, source_target_pairs={{0,16},{16,0},{32,48},{48,32},{64,80},{80,64},{96,112},{112,96},{1... | collective-permute-start | bytes 196616 | tf_op jit(solution)/shard_map/ppermute | solution.py:311

commit v3 on v2

--- a/solution.py
+++ b/solution.py
@@ -70,7 +70,7 @@
 
 def leaf_kernel(
     w_ref, inv_hbm, rhs_hbm, blk_hbm, out_hbm, m3_hbm,
-    t1_ref, t2_ref, t3_ref, o_ref, sent_ref, a8_hbm,
+    t1_ref, t2_ref, t3_ref, o_ref, a8_hbm,
     inv, rhs, blk, out, y, masked, m3, folded, sems, sends,
 ):
     copies = []
@@ -103,8 +103,6 @@
             masked[t, :, j * 256 : (j + 1) * 256] = block * w_ref[j, t].astype(F32).astype(BF16)
     for t, into in enumerate((t1_ref, t2_ref, t3_ref, o_ref)):
         into[...] = dot(masked[t], y[...]).astype(into.dtype)
-    for half in range(2):
-        sent_ref[:, half * 128 : (half + 1) * 128] = own_and_other(t1_ref, half)[1].astype(BF16)
     for copy in blocks:
         copy.wait()
 
@@ -123,9 +121,9 @@
         leaf_kernel,
         name="leaf",
         in_specs=[pl.BlockSpec(memory_space=pltpu.SMEM)] + [pl.BlockSpec(memory_space=pl.ANY)] * 5,
-        out_specs=[pl.BlockSpec(memory_space=pltpu.VMEM)] * 5 + [pl.BlockSpec(memory_space=pl.ANY)],
+        out_specs=[pl.BlockSpec(memory_space=pltpu.VMEM)] * 4 + [pl.BlockSpec(memory_space=pl.ANY)],
         out_shape=[
-            pltpu.VMEM((256, 512), BF16), full, full, full, pltpu.VMEM((256, 256), BF16),
+            pltpu.VMEM((256, 512), BF16), full, full, full,
             pltpu.HBM((8, 384, 128), BF16),
         ],
         scratch_shapes=[
@@ -145,7 +143,7 @@
     )(*map(in_hbm, (weights, inverse, rhs, blocks, outer, m3)))
 
 
-def first_kernel(t1_ref, t2_ref, t3_ref, o_ref, m1_ref, m1r_ref, t2n_ref, t3n_ref, on_ref, d1_ref, sent_ref, kept_ref, one, shares):
+def first_kernel(t1_ref, t2_ref, t3_ref, o_ref, m1_ref, m1r_ref, t2n_ref, t3n_ref, on_ref, d1_ref, kept_ref, near_ref, far_ref, ring_ref, one, shares):
     row = lax.axis_index("srow")
     own = pl.multiple_of((row & 1) * 128, 128)
     other = pl.multiple_of(128 - (row & 1) * 128, 128)
@@ -162,20 +160,26 @@
         shares[2 * t] = join_halves(first, second, False)
         shares[2 * t + 1] = join_halves(first, second, True)
     place = row & 3
-    for i in range(2):
-        kept_ref[i] = shares[place ^ i].astype(BF16)
-        sent_ref[i] = shares[place ^ 3 ^ i].astype(BF16)
+    for half in range(2):
+        near_ref[:, half * 128 : (half + 1) * 128] = own_and_other(t1_ref, half)[1].astype(BF16)
+    near_ref[:, 256:] = shares[place ^ 1].astype(BF16)
+    kept_ref[...] = shares[place]
+    far_ref[...] = shares[place ^ 2].astype(BF16)
+    ring_ref[...] = shares[place ^ 3].astype(BF16)
     t3n_ref[...] = t3_ref[...] - under[256:512]
     on_ref[...] = o_ref[...] - under[512:]
 
 
 def first_level(t1, t2, t3, o, m1, m1r):
     full = pltpu.VMEM((256, 512), F32)
-    two = pltpu.VMEM((2, 256, 128), BF16)
+    share = pltpu.VMEM((256, 128), BF16)
     return pl.pallas_call(
         first_kernel,
         name="first",
-        out_shape=[full, full, full, pltpu.VMEM((256, 256), BF16), two, two],
+        out_shape=[
+            full, full, full, pltpu.VMEM((256, 256), BF16),
+            pltpu.VMEM((256, 128), F32), pltpu.VMEM((256, 384), BF16), share, share,
+        ],
         scratch_shapes=[pltpu.VMEM((3, 256, 256), BF16), pltpu.VMEM((4, 256, 128), F32)],
         input_output_aliases={1: 0, 2: 1, 3: 2},
         compiler_params=pltpu.CompilerParams(vmem_limit_bytes=TRANSFORM_BYTES),
@@ -239,22 +243,7 @@
     low = low_lanes((8, 128))
     for p in range(16):
         upper, lower = v[p * 16 : p * 16 + 8, :], v[p * 16 + 8 : p * 16 + 16, :]
-        out_ref[p] = jnp.where(low, pltpu.roll(upper, 64, 1), lower)
-
-
-def middle_kernel(kept_ref, came_ref, own_ref, sent_ref):
-    own_ref[...] = kept_ref[0].astype(F32) + came_ref[0].astype(F32)
-    sent_ref[...] = (kept_ref[1].astype(F32) + came_ref[1].astype(F32)).astype(BF16)
-
-
-def middle_sums(kept, came):
-    return pl.pallas_call(
-        middle_kernel,
-        name="middle",
-        out_shape=[pltpu.VMEM((256, 128), F32), pltpu.VMEM((256, 128), BF16)],
-        compiler_params=pltpu.CompilerParams(vmem_limit_bytes=SMALL_BYTES),
-        cost_estimate=pl.CostEstimate(flops=1, bytes_accessed=1, transcendentals=0),
-    )(in_vmem(kept), in_vmem(came))
+        out_ref[p] = jnp.where(low, pltpu.roll(upper, 64, 1), lower).astype(BF16)
 
 
 def third_level(r8):
@@ -263,35 +252,36 @@
         name="third",
         out_shape=[
             jax.ShapeDtypeStruct((64, 256), BF16),
-            pltpu.VMEM((16, 8, 128), F32),
+            pltpu.VMEM((16, 8, 128), BF16),
         ],
         scratch_shapes=[pltpu.VMEM((256, 256), BF16), pltpu.VMEM((256, 256), BF16), pltpu.VMEM((256, 128), F32)],
         compiler_params=pltpu.CompilerParams(vmem_limit_bytes=SMALL_BYTES),
-        cost_estimate=pl.CostEstimate(flops=70_000_000, bytes_accessed=1_300_000, transcendentals=0),
+        cost_estimate=pl.CostEstimate(flops=70_000_000, bytes_accessed=1, transcendentals=0),
     )(in_vmem(r8))
 
 
-def lower_kernel(t1_ref, came1_ref, own2_ref, came2_ref, d1_ref, d2_ref, x1_ref, x2_ref):
+def lower_kernel(t1_ref, kept_ref, near_ref, far_ref, ring_ref, d1_ref, d2_ref, x1_ref, x2_ref):
     kept_one = jnp.concatenate([own_and_other(t1_ref, half)[0] for half in range(2)], axis=1)
-    sum_one = kept_one + came1_ref[...].astype(F32)
-    x1_ref[...] = (-dot_wide(d1_ref[...], sum_one)).astype(BF16)
-    x2_ref[...] = (-dot_wide(d2_ref[...], own2_ref[...] + came2_ref[...].astype(F32))).astype(BF16)
-
-
-def lower_levels(t1, came1, own2, came2, d1, d2):
+    x1_ref[...] = (-dot_wide(d1_ref[...], kept_one + near_ref[:, :256].astype(F32))).astype(BF16)
+    sum_two = kept_ref[...] + near_ref[:, 256:].astype(F32)
+    sum_two = sum_two + far_ref[...].astype(F32) + ring_ref[...].astype(F32)
+    x2_ref[...] = (-dot_wide(d2_ref[...], sum_two)).astype(BF16)
+
+
+def lower_levels(t1, kept, near, far, ring, d1, d2):
     return pl.pallas_call(
         lower_kernel,
         name="lower",
         out_shape=[jax.ShapeDtypeStruct((256, 256), BF16), jax.ShapeDtypeStruct((256, 128), BF16)],
         compiler_params=pltpu.CompilerParams(vmem_limit_bytes=SMALL_BYTES),
         cost_estimate=pl.CostEstimate(flops=1, bytes_accessed=1, transcendentals=0),
-    )(*map(in_vmem, (t1, came1, own2, came2, d1, d2)))
+    )(*map(in_vmem, (t1, kept, near, far, ring, d1, d2)))
 
 
 def final_kernel(r_ref, after_ref, out_ref):
-    total = r_ref[0]
+    total = r_ref[0].astype(F32)
     for k in range(1, 16):
-        total = total + r_ref[k]
+        total = total + r_ref[k].astype(F32)
     out_ref[0:8, :] = total[:, :64]
     out_ref[8:16, :] = pltpu.roll(total, 64, 1)[:, :64]
 
@@ -318,17 +308,15 @@
     m1r = swap(m1, 1)
     m2 = spread(jnp.transpose(level_two[:, 0], (1, 0, 2)))
     m2 = lax.all_to_all(m2, "srow", 0, 0, axis_index_groups=GROUPS_4, tiled=True)
-    t1, t2, t3, o, sent1, a8 = leaf_terms(
+    t1, t2, t3, o, a8 = leaf_terms(
         leaf_targets[0, 0], leaf_inverse[0, 0], leaf_rhs[0, 0], leaf_blocks[0, 0], leaf_outer[0, 0], m3
     )
-    came1 = swap(sent1, 1)
-    t2, t3, o, d1, sent2, kept2 = first_level(t1, t2, t3, o, m1, m1r)
+    t2, t3, o, d1, kept, near, far, ring = first_level(t1, t2, t3, o, m1, m1r)
     a8, d2 = second_level(t2, t3, o, m2, a8)
     r8 = lax.all_to_all(a8, "srow", 0, 0, axis_index_groups=GROUPS_8, tiled=True)
     x3, parts = third_level(r8)
-    own2, sent2 = middle_sums(kept2, swap(sent2, 3))
     received = lax.all_to_all(parts, "scol", 0, 0, tiled=True)
-    x1, x2 = lower_levels(t1, came1, own2, swap(sent2, 1), d1, d2)
+    x1, x2 = lower_levels(t1, kept, swap(near, 1), swap(far, 2), swap(ring, 3), d1, d2)
     outer_update = final_sum(received, x2)
     return (x1[:, None, :], x2[:, None, :], jnp.transpose(x3)[:, None, :], outer_update)
 

time: 57.4 us -> 56.1 us (0.977)
  starting transfers between devices: 37.6 us -> 36.3 us
    all_to_all x1, waiting for transfers between devices: 1.12 us -> 6.26 us  [shards(): received = lax.all_to_all(parts, 'scol', 0, 0, tiled=True)]
    ppermute x4, waiting for transfers between devices: 3.24 us -> 0.01 us  [swap(): return lax.ppermute(block, 'srow', [(i, i ^ flip) for i in range(32)])]
    all_to_all x1, starting transfers between devices: 16.2 us -> 14 us  [shards(): received = lax.all_to_all(parts, 'scol', 0, 0, tiled=True)]
    all_to_all x1, waiting for transfers between devices: 1.88 us -> 0.01 us  [shards(): lax.all_to_all(a8, 'srow', 0, 0, axis_index_groups=GROUPS_8, tiled=True)]
    ppermute x4, starting transfers between devices: 12.7 us -> 13.5 us  [swap(): return lax.ppermute(block, 'srow', [(i, i ^ flip) for i in range(32)])]
  transfers between devices with their start and end apart: 7 -> 7, of which waited for: 4 -> 2; matrix products, arithmetic and copies ran while one was open for 0% -> 0% of each run, Pallas kernels for 16% -> 16%
where the time goes in v3:
time: 56.1 us; the launch traced here: 55.7 us
  starting transfers between devices  36.3 us (65%)
  Pallas kernels  11.2 us (20%)
  waiting for transfers between devices  6.55 us (12%)
  local copies, waits for them, and re-layouts  0.89 us (2%)
  between operations  0.75 us (1%)
    all_to_all x1, starting transfers between devices, shards(): received = lax.all_to_all(parts, 'scol', 0, 0, tiled=True)  14 us
    ppermute x4, starting transfers between devices, swap(): return lax.ppermute(block, 'srow', [(i, i ^ flip) for i in range(32)])  13.5 us
    all_to_all x1, waiting for transfers between devices, shards(): received = lax.all_to_all(parts, 'scol', 0, 0, tiled=True)  6.26 us
    all_to_all x1, starting transfers between devices, shards(): lax.all_to_all(a8, 'srow', 0, 0, axis_index_groups=GROUPS_8, tiled=True)  5.02 us
    pallas_call x1, Pallas kernels, leaf_terms(): pl.pallas_call(leaf_kernel, name='leaf', in_specs=[pl.BlockSpec(memory_sp...  4.46 us
    all_to_all x1, starting transfers between devices, shards(): lax.all_to_all(m2, 'srow', 0, 0, axis_index_groups=GROUPS_4, tiled=True)  3.73 us
    pallas_call x1, Pallas kernels, first_level(): pl.pallas_call(first_kernel, name='first', out_shape=[full, full, full, p...  1.46 us
    pallas_call x1, Pallas kernels, second_level(): pl.pallas_call(second_kernel, name='second', in_specs=[pl.BlockSpec(memor...  1.45 us
  transfers between devices with their start and end apart: 7, of which 2 were waited for; matrix products, arithmetic and copies ran while one was open for 0% of the time, Pallas kernels for 16%

profile of v3, /device:TPU:1, one launch (start us, length us, event | category | flops | bytes accessed | tf_op | source)
XLA Modules:
  0.0 55.7 jit_solution(677201369258420886)
XLA Ops:
  0.6 4.0 %collective-permute-start = (bf16[128,4,256]{2,1,0:T(4,128)(2,1)}, bf16[128,4,256]{2,1,0:T(4,128)(2,1)S(1)}, u32[]{:S(2)}, u32[]{:S(2)}) collective-permute-start(bf16[128,4,256]{2,1,0:T(4,128)(2,1)} %bitcast.16), channel_id=1, source_target_pairs={{0,16},{16,0},{32,48},{48,32},{64,80},{80,64},{96,112},{112,96},{1... | collective-permute-start | bytes 786440 | tf_op jit(solution)/shard_map/ppermute | solution.py:301
  4.6 0.0 copy-start
  4.6 0.9 %copy-done = bf16[64,1,3,256]{3,0,2,1:T(8,128)(2,1)S(1)} copy-done((bf16[64,1,3,256]{3,0,2,1:T(8,128)(2,1)S(1)}, bf16[64,1,3,256]{3,0,2,1:T(8,128)(2,1)}, u32[]{:S(2)}) %copy-start) | copy-done | bytes 98328
  5.5 0.8 %spread.1 = bf16[4,3,64,256]{3,2,1,0:T(8,128)(2,1)} custom-call(bf16[3,64,256]{2,1,0:T(8,128)(2,1)S(1)} %bitcast.15), custom_call_target="tpu_custom_call" | custom-call | flops 1000 | bytes 500000 | tf_op jit(solution)/shard_map/spread/pallas_call | solution.py:59
  6.3 3.7 %all-to-all-start = ((bf16[4,3,64,256]{3,2,1,0:T(8,128)(2,1)}), bf16[4,3,64,256]{3,2,1,0:T(8,128)(2,1)S(1)}, u32[]{:S(2)}, u32[]{:S(2)}) async-start(bf16[4,3,64,256]{3,2,1,0:T(8,128)(2,1)} %spread.1), calls=%async_computation | async-start | bytes 786432 | tf_op jit(solution)/shard_map/all_to_all | solution.py:310
  10.0 0.0 copy-start.1
  10.0 4.5 %leaf.1 = (bf16[256,512]{1,0:T(8,128)(2,1)S(1)}, f32[256,512]{1,0:T(8,128)S(1)}, f32[256,512]{1,0:T(8,128)S(1)}, f32[256,512]{1,0:T(8,128)S(1)}, bf16[8,384,128]{2,1,0:T(8,128)(2,1)}) custom-call(s32[4,4]{1,0:T(4,128)} %bitcast.26, bf16[4,256,256]{2,1,0:T(8,128)(2,1)} %bitcast.21, bf16[4,256,512]{2,1,0:T(8,128)(2,1)} %bitcast.20, ...), custom_call_target="tpu_custom_call" | custom-call | flops 1342177280 | bytes 6000000 | tf_op jit(solution)/shard_map/leaf/pallas_call | solution.py:120
  14.5 0.0 collective-permute-done.m1r_ref
  14.5 0.0 copy-done.1
  14.5 1.5 %first.1 = (f32[256,512]{1,0:T(8,128)S(1)}, f32[256,512]{1,0:T(8,128)S(1)}, f32[256,512]{1,0:T(8,128)S(1)}, bf16[256,256]{1,0:T(8,128)(2,1)S(1)}, f32[256,128]{1...) custom-call(bf16[256,512]{1,0:T(8,128)(2,1)S(1)} %get-tuple-element., ...), custom_call_target="tpu_custom_call", output_to_operand_aliasing={{0}: (1, {}), {1}: (2, {}), {2}: (3, {})} | custom-call | flops 5000000000 | bytes 3000000 | tf_op jit(solution)/shard_map/first/pallas_call | solution.py:176
  16.0 0.3 all-to-all-done.m2_ref
  16.2 1.4 %second.1 = (bf16[8,384,128]{2,1,0:T(8,128)(2,1)}, bf16[256,256]{1,0:T(8,128)(2,1)S(1)}) custom-call(f32[256,512]{1,0:T(8,128)S(1)} %get-tuple-element.32.t2_ref, f32[256,512]{1,0:T(8,128)S(1)} %get-tuple-element.33.t3_ref, f32[256,512]{1,0:T(8,128)S(1)} %get-tuple-element.34.o_ref, ...), custom_call_target="tpu_custom_call", output_to_operand_aliasing={{0}: (4, {})} | custom-call | flops 200000000 | bytes 3000000 | tf_op jit(solution)/shard_map/second/pallas_call | solution.py:213
  17.7 5.0 %all-to-all-start.1 = ((bf16[8,384,128]{2,1,0:T(8,128)(2,1)}), bf16[8,384,128]{2,1,0:T(8,128)(2,1)S(1)}, u32[]{:S(2)}, u32[]{:S(2)}) async-start(bf16[8,384,128]{2,1,0:T(8,128)(2,1)} %get-tuple-element.39), calls=%async_computation.1 | async-start | bytes 1572864 | tf_op jit(solution)/shard_map/all_to_all | solution.py:316
  22.7 3.4 %collective-permute-start.1 = (bf16[256,384]{1,0:T(8,128)(2,1)S(1)}, bf16[256,384]{1,0:T(8,128)(2,1)S(1)}, u32[]{:S(2)}, u32[]{:S(2)}) collective-permute-start(bf16[256,384]{1,0:T(8,128)(2,1)S(1)} %get-tuple-element.28), channel_id=1, source_target_pairs={{0,16},{16,0},{32,48},{48,32},{64,80},{80,64},{96,112},{112,96},{1... | collective-permute-start | bytes 589832 | tf_op jit(solution)/shard_map/ppermute | solution.py:301
  26.1 4.3 %collective-permute-start.2 = (bf16[256,128]{1,0:T(8,128)(2,1)S(1)}, bf16[256,128]{1,0:T(8,128)(2,1)S(1)}, u32[]{:S(2)}, u32[]{:S(2)}) collective-permute-start(bf16[256,128]{1,0:T(8,128)(2,1)S(1)} %get-tuple-element.29), channel_id=1, source_target_pairs={{0,32},{16,48},{32,0},{48,16},{64,96},{80,112},{96,64},{112,80},{1... | collective-permute-start | bytes 196616 | tf_op jit(solution)/shard_map/ppermute | solution.py:301
  30.4 1.9 %collective-permute-start.3 = (bf16[256,128]{1,0:T(8,128)(2,1)S(1)}, bf16[256,128]{1,0:T(8,128)(2,1)S(1)}, u32[]{:S(2)}, u32[]{:S(2)}) collective-permute-start(bf16[256,128]{1,0:T(8,128)(2,1)S(1)} %get-tuple-element.30), channel_id=1, source_target_pairs={{0,48},{16,32},{32,16},{48,0},{64,112},{80,96},{96,80},{112,64},{1... | collective-permute-start | bytes 196616 | tf_op jit(solution)/shard_map/ppermute | solution.py:301
  32.3 0.0 all-to-all-done.1.r8_ref
  32.3 1.2 %third.1 = (bf16[64,256]{1,0:T(8,128)(2,1)}, bf16[16,8,128]{2,1,0:T(8,128)(2,1)}) custom-call(bf16[8,384,128]{2,1,0:T(8,128)(2,1)S(1)} %all-to-all-done.1.r8_ref), custom_call_target="tpu_custom_call" | custom-call | flops 70000000 | bytes 1 | tf_op jit(solution)/shard_map/third/pallas_call | solution.py:250
  33.6 14.0 %all-to-all-start.2 = ((bf16[16,8,128]{2,1,0:T(8,128)(2,1)}), bf16[16,8,128]{2,1,0:T(8,128)(2,1)S(1)}, u32[]{:S(2)}, u32[]{:S(2)}) async-start(bf16[16,8,128]{2,1,0:T(8,128)(2,1)} %get-tuple-element.41), calls=%async_computation.2 | async-start | bytes 65536 | tf_op jit(solution)/shard_map/all_to_all | solution.py:318
  47.6 0.0 collective-permute-done.2.far_ref
  47.6 0.0 collective-permute-done.3.ring_ref
  47.6 0.0 collective-permute-done.1.near_ref
  47.6 1.1 %lower.1 = (bf16[256,256]{1,0:T(8,128)(2,1)}, bf16[256,128]{1,0:T(8,128)(2,1)}) custom-call(bf16[256,512]{1,0:T(8,128)(2,1)S(1)} %get-tuple-element.23.t1_ref, f32[256,128]{1,0:T(8,128)S(1)} %get-tuple-element.27.kept_ref, bf16[256,384]{1,0:T(8,128)(2,1)S(1)} %collective-permute-done.1.near_ref, bf16[256,128]{1,0:T(8,128)(2,1)S(1)} %collective-permute-done.2.far_ref, ...), custom_call_target="tpu_custom_call" | custom-call | flops 1 | bytes 1 | tf_op jit(solution)/shard_map/lower/pallas_call | solution.py:272
  48.7 6.3 %all-to-all-done.2.r_ref = bf16[16,8,128]{2,1,0:T(8,128)(2,1)S(1)} async-done(((bf16[16,8,128]{2,1,0:T(8,128)(2,1)}), bf16[16,8,128]{2,1,0:T(8,128)(2,1)S(1)}, u32[]{:S(2)}, u32[]{:S(2)}) %all-to-all-start.2) | async-done | bytes 32800 | tf_op jit(solution)/shard_map/all_to_all | solution.py:318
  55.0 0.7 %final.1 = f32[16,64]{1,0:T(8,128)} custom-call(bf16[16,8,128]{2,1,0:T(8,128)(2,1)S(1)} %all-to-all-done.2.r_ref, bf16[256,128]{1,0:T(8,128)(2,1)} %get-tuple-element.38.after_ref), custom_call_target="tpu_custom_call" | custom-call | flops 20000 | bytes 40000 | tf_op jit(solution)/shard_map/final/pallas_call | solution.py:290
Async XLA Ops:
  0.6 13.9 %collective-permute-start = (bf16[128,4,256]{2,1,0:T(4,128)(2,1)}, bf16[128,4,256]{2,1,0:T(4,128)(2,1)S(1)}, u32[]{:S(2)}, u32[]{:S(2)}) collective-permute-start(bf16[128,4,256]{2,1,0:T(4,128)(2,1)} %bitcast.16), channel_id=1, source_target_pairs={{0,16},{16,0},{32,48},{48,32},{64,80},{80,64},{96,112},{112,96},{1... | collective-permute-start | bytes 786440 | tf_op jit(solution)/shard_map/ppermute | solution.py:301
  4.6 0.9 %copy-start = (bf16[64,1,3,256]{3,0,2,1:T(8,128)(2,1)S(1)}, bf16[64,1,3,256]{3,0,2,1:T(8,128)(2,1)}, u32[]{:S(2)}) copy-start(bf16[64,1,3,256]{3,0,2,1:T(8,128)(2,1)} %param.14) | copy-start | bytes 294916
  6.3 10.0 %all-to-all-start = ((bf16[4,3,64,256]{3,2,1,0:T(8,128)(2,1)}), bf16[4,3,64,256]{3,2,1,0:T(8,128)(2,1)S(1)}, u32[]{:S(2)}, u32[]{:S(2)}) async-start(bf16[4,3,64,256]{3,2,1,0:T(8,128)(2,1)} %spread.1), calls=%async_computation | async-start | bytes 786432 | tf_op jit(solution)/shard_map/all_to_all | solution.py:310
  10.0 4.5 %copy-start.1 = (bf16[128,1,4,256]{3,2,1,0:T(4,128)(2,1)S(1)}, bf16[128,1,4,256]{3,2,1,0:T(4,128)(2,1)}, u32[]{:S(2)}) copy-start(bf16[128,1,4,256]{3,2,1,0:T(4,128)(2,1)} %param.13) | copy-start | bytes 786436
  17.7 14.6 %all-to-all-start.1 = ((bf16[8,384,128]{2,1,0:T(8,128)(2,1)}), bf16[8,384,128]{2,1,0:T(8,128)(2,1)S(1)}, u32[]{:S(2)}, u32[]{:S(2)}) async-start(bf16[8,384,128]{2,1,0:T(8,128)(2,1)} %get-tuple-element.39), calls=%async_computation.1 | async-start | bytes 1572864 | tf_op jit(solution)/shard_map/all_to_all | solution.py:316
  22.7 24.9 %collective-permute-start.1 = (bf16[256,384]{1,0:T(8,128)(2,1)S(1)}, bf16[256,384]{1,0:T(8,128)(2,1)S(1)}, u32[]{:S(2)}, u32[]{:S(2)}) collective-permute-start(bf16[256,384]{1,0:T(8,128)(2,1)S(1)} %get-tuple-element.28), channel_id=1, source_target_pairs={{0,16},{16,0},{32,48},{48,32},{64,80},{80,64},{96,112},{112,96},{1... | collective-permute-start | bytes 589832 | tf_op jit(solution)/shard_map/ppermute | solution.py:301
  26.1 21.5 %collective-permute-start.2 = (bf16[256,128]{1,0:T(8,128)(2,1)S(1)}, bf16[256,128]{1,0:T(8,128)(2,1)S(1)}, u32[]{:S(2)}, u32[]{:S(2)}) collective-permute-start(bf16[256,128]{1,0:T(8,128)(2,1)S(1)} %get-tuple-element.29), channel_id=1, source_target_pairs={{0,32},{16,48},{32,0},{48,16},{64,96},{80,112},{96,64},{112,80},{1... | collective-permute-start | bytes 196616 | tf_op jit(solution)/shard_map/ppermute | solution.py:301
  30.4 17.2 %collective-permute-start.3 = (bf16[256,128]{1,0:T(8,128)(2,1)S(1)}, bf16[256,128]{1,0:T(8,128)(2,1)S(1)}, u32[]{:S(2)}, u32[]{:S(2)}) collective-permute-start(bf16[256,128]{1,0:T(8,128)(2,1)S(1)} %get-tuple-element.30), channel_id=1, source_target_pairs={{0,48},{16,32},{32,16},{48,0},{64,112},{80,96},{96,80},{112,64},{1... | collective-permute-start | bytes 196616 | tf_op jit(solution)/shard_map/ppermute | solution.py:301
  33.6 21.4 %all-to-all-start.2 = ((bf16[16,8,128]{2,1,0:T(8,128)(2,1)}), bf16[16,8,128]{2,1,0:T(8,128)(2,1)S(1)}, u32[]{:S(2)}, u32[]{:S(2)}) async-start(bf16[16,8,128]{2,1,0:T(8,128)(2,1)} %get-tuple-element.41), calls=%async_computation.2 | async-start | bytes 65536 | tf_op jit(solution)/shard_map/all_to_all | solution.py:318

commit v4 on v3

--- a/solution.py
+++ b/solution.py
@@ -183,7 +183,7 @@
         scratch_shapes=[pltpu.VMEM((3, 256, 256), BF16), pltpu.VMEM((4, 256, 128), F32)],
         input_output_aliases={1: 0, 2: 1, 3: 2},
         compiler_params=pltpu.CompilerParams(vmem_limit_bytes=TRANSFORM_BYTES),
-        cost_estimate=pl.CostEstimate(flops=5_000_000_000, bytes_accessed=3_000_000, transcendentals=0),
+        cost_estimate=pl.CostEstimate(flops=270_000_000, bytes_accessed=3_000_000, transcendentals=0),
     )(*map(in_vmem, (t1, t2, t3, o, m1, m1r)))
 
 

time: 56.1 us -> 59.5 us (1.061)
  starting transfers between devices: 36.3 us -> 39.9 us
    all_to_all x1, starting transfers between devices: 5.02 us -> 8.1 us  [shards(): lax.all_to_all(a8, 'srow', 0, 0, axis_index_groups=GROUPS_8, tiled=True)]
    all_to_all x1, starting transfers between devices: 3.73 us -> 4.85 us  [shards(): lax.all_to_all(m2, 'srow', 0, 0, axis_index_groups=GROUPS_4, tiled=True)]
  transfers between devices with their start and end apart: 7 -> 7, of which waited for: 2 -> 1; matrix products, arithmetic and copies ran while one was open for 0% -> 0% of each run, Pallas kernels for 16% -> 14%
where the time goes in v4:
time: 59.5 us; the launch traced here: 59 us
  starting transfers between devices  39.9 us (67%)
  Pallas kernels  11.2 us (19%)
  waiting for transfers between devices  6.28 us (11%)
  local copies, waits for them, and re-layouts  0.89 us (1%)
  between operations  0.76 us (1%)
    all_to_all x1, starting transfers between devices, shards(): received = lax.all_to_all(parts, 'scol', 0, 0, tiled=True)  14 us
    ppermute x4, starting transfers between devices, swap(): return lax.ppermute(block, 'srow', [(i, i ^ flip) for i in range(32)])  12.9 us
    all_to_all x1, starting transfers between devices, shards(): lax.all_to_all(a8, 'srow', 0, 0, axis_index_groups=GROUPS_8, tiled=True)  8.1 us
    all_to_all x1, waiting for transfers between devices, shards(): received = lax.all_to_all(parts, 'scol', 0, 0, tiled=True)  6.26 us
    all_to_all x1, starting transfers between devices, shards(): lax.all_to_all(m2, 'srow', 0, 0, axis_index_groups=GROUPS_4, tiled=True)  4.85 us
    pallas_call x1, Pallas kernels, leaf_terms(): pl.pallas_call(leaf_kernel, name='leaf', in_specs=[pl.BlockSpec(memory_sp...  4.47 us
    pallas_call x1, Pallas kernels, first_level(): pl.pallas_call(first_kernel, name='first', out_shape=[full, full, full, p...  1.46 us
    pallas_call x1, Pallas kernels, second_level(): pl.pallas_call(second_kernel, name='second', in_specs=[pl.BlockSpec(memor...  1.45 us
  transfers between devices with their start and end apart: 7, of which 1 were waited for; matrix products, arithmetic and copies ran while one was open for 0% of the time, Pallas kernels for 14%

profile of v4, /device:TPU:1, one launch (start us, length us, event | category | flops | bytes accessed | tf_op | source)
XLA Modules:
  0.0 59.0 jit_solution(2648128772865497321)
XLA Ops:
  0.6 0.0 copy-start.1
  0.6 0.9 %copy-done.1 = bf16[64,1,3,256]{3,0,2,1:T(8,128)(2,1)S(1)} copy-done((bf16[64,1,3,256]{3,0,2,1:T(8,128)(2,1)S(1)}, bf16[64,1,3,256]{3,0,2,1:T(8,128)(2,1)}, u32[]{:S(2)}) %copy-start.1) | copy-done | bytes 98328
  1.5 0.8 %spread.1 = bf16[4,3,64,256]{3,2,1,0:T(8,128)(2,1)} custom-call(bf16[3,64,256]{2,1,0:T(8,128)(2,1)S(1)} %bitcast.17), custom_call_target="tpu_custom_call" | custom-call | flops 1000 | bytes 500000 | tf_op jit(solution)/shard_map/spread/pallas_call | solution.py:59
  2.3 4.9 %all-to-all-start = ((bf16[4,3,64,256]{3,2,1,0:T(8,128)(2,1)}), bf16[4,3,64,256]{3,2,1,0:T(8,128)(2,1)S(1)}, u32[]{:S(2)}, u32[]{:S(2)}) async-start(bf16[4,3,64,256]{3,2,1,0:T(8,128)(2,1)} %spread.1), calls=%async_computation | async-start | bytes 786432 | tf_op jit(solution)/shard_map/all_to_all | solution.py:310
  7.2 3.4 %collective-permute-start = (bf16[128,4,256]{2,1,0:T(4,128)(2,1)}, bf16[128,4,256]{2,1,0:T(4,128)(2,1)S(1)}, u32[]{:S(2)}, u32[]{:S(2)}) collective-permute-start(bf16[128,4,256]{2,1,0:T(4,128)(2,1)} %bitcast.15), channel_id=1, source_target_pairs={{0,16},{16,0},{32,48},{48,32},{64,80},{80,64},{96,112},{112,96},{1... | collective-permute-start | bytes 786440 | tf_op jit(solution)/shard_map/ppermute | solution.py:301
  10.6 0.0 copy-start
  10.6 4.5 %leaf.1 = (bf16[256,512]{1,0:T(8,128)(2,1)S(1)}, f32[256,512]{1,0:T(8,128)S(1)}, f32[256,512]{1,0:T(8,128)S(1)}, f32[256,512]{1,0:T(8,128)S(1)}, bf16[8,384,128]{2,1,0:T(8,128)(2,1)}) custom-call(s32[4,4]{1,0:T(4,128)} %bitcast.26, bf16[4,256,256]{2,1,0:T(8,128)(2,1)} %bitcast.21, bf16[4,256,512]{2,1,0:T(8,128)(2,1)} %bitcast.20, ...), custom_call_target="tpu_custom_call" | custom-call | flops 1342177280 | bytes 6000000 | tf_op jit(solution)/shard_map/leaf/pallas_call | solution.py:120
  15.0 0.0 collective-permute-done.m1r_ref
  15.0 0.0 copy-done
  15.1 1.5 %first.1 = (f32[256,512]{1,0:T(8,128)S(1)}, f32[256,512]{1,0:T(8,128)S(1)}, f32[256,512]{1,0:T(8,128)S(1)}, bf16[256,256]{1,0:T(8,128)(2,1)S(1)}, f32[256,128]{1...) custom-call(bf16[256,512]{1,0:T(8,128)(2,1)S(1)} %get-tuple-element., ...), custom_call_target="tpu_custom_call", output_to_operand_aliasing={{0}: (1, {}), {1}: (2, {}), {2}: (3, {})} | custom-call | flops 270000000 | bytes 3000000 | tf_op jit(solution)/shard_map/first/pallas_call | solution.py:176
  16.5 0.0 all-to-all-done.m2_ref
  16.5 1.5 %second.1 = (bf16[8,384,128]{2,1,0:T(8,128)(2,1)}, bf16[256,256]{1,0:T(8,128)(2,1)S(1)}) custom-call(f32[256,512]{1,0:T(8,128)S(1)} %get-tuple-element.32.t2_ref, f32[256,512]{1,0:T(8,128)S(1)} %get-tuple-element.33.t3_ref, f32[256,512]{1,0:T(8,128)S(1)} %get-tuple-element.34.o_ref, ...), custom_call_target="tpu_custom_call", output_to_operand_aliasing={{0}: (4, {})} | custom-call | flops 200000000 | bytes 3000000 | tf_op jit(solution)/shard_map/second/pallas_call | solution.py:213
  18.0 8.1 %all-to-all-start.1 = ((bf16[8,384,128]{2,1,0:T(8,128)(2,1)}), bf16[8,384,128]{2,1,0:T(8,128)(2,1)S(1)}, u32[]{:S(2)}, u32[]{:S(2)}) async-start(bf16[8,384,128]{2,1,0:T(8,128)(2,1)} %get-tuple-element.39), calls=%async_computation.1 | async-start | bytes 1572864 | tf_op jit(solution)/shard_map/all_to_all | solution.py:316
  26.1 3.4 %collective-permute-start.1 = (bf16[256,384]{1,0:T(8,128)(2,1)S(1)}, bf16[256,384]{1,0:T(8,128)(2,1)S(1)}, u32[]{:S(2)}, u32[]{:S(2)}) collective-permute-start(bf16[256,384]{1,0:T(8,128)(2,1)S(1)} %get-tuple-element.28), channel_id=1, source_target_pairs={{0,16},{16,0},{32,48},{48,32},{64,80},{80,64},{96,112},{112,96},{1... | collective-permute-start | bytes 589832 | tf_op jit(solution)/shard_map/ppermute | solution.py:301
  29.5 4.3 %collective-permute-start.2 = (bf16[256,128]{1,0:T(8,128)(2,1)S(1)}, bf16[256,128]{1,0:T(8,128)(2,1)S(1)}, u32[]{:S(2)}, u32[]{:S(2)}) collective-permute-start(bf16[256,128]{1,0:T(8,128)(2,1)S(1)} %get-tuple-element.29), channel_id=1, source_target_pairs={{0,32},{16,48},{32,0},{48,16},{64,96},{80,112},{96,64},{112,80},{1... | collective-permute-start | bytes 196616 | tf_op jit(solution)/shard_map/ppermute | solution.py:301
  33.8 1.9 %collective-permute-start.3 = (bf16[256,128]{1,0:T(8,128)(2,1)S(1)}, bf16[256,128]{1,0:T(8,128)(2,1)S(1)}, u32[]{:S(2)}, u32[]{:S(2)}) collective-permute-start(bf16[256,128]{1,0:T(8,128)(2,1)S(1)} %get-tuple-element.30), channel_id=1, source_target_pairs={{0,48},{16,32},{32,16},{48,0},{64,112},{80,96},{96,80},{112,64},{1... | collective-permute-start | bytes 196616 | tf_op jit(solution)/shard_map/ppermute | solution.py:301
  35.7 0.0 all-to-all-done.1.r8_ref
  35.7 1.2 %third.1 = (bf16[64,256]{1,0:T(8,128)(2,1)}, bf16[16,8,128]{2,1,0:T(8,128)(2,1)}) custom-call(bf16[8,384,128]{2,1,0:T(8,128)(2,1)S(1)} %all-to-all-done.1.r8_ref), custom_call_target="tpu_custom_call" | custom-call | flops 70000000 | bytes 1 | tf_op jit(solution)/shard_map/third/pallas_call | solution.py:250
  37.0 14.0 %all-to-all-start.2 = ((bf16[16,8,128]{2,1,0:T(8,128)(2,1)}), bf16[16,8,128]{2,1,0:T(8,128)(2,1)S(1)}, u32[]{:S(2)}, u32[]{:S(2)}) async-start(bf16[16,8,128]{2,1,0:T(8,128)(2,1)} %get-tuple-element.41), calls=%async_computation.2 | async-start | bytes 65536 | tf_op jit(solution)/shard_map/all_to_all | solution.py:318
  51.0 0.0 collective-permute-done.2.far_ref
  51.0 0.0 collective-permute-done.3.ring_ref
  51.0 0.0 collective-permute-done.1.near_ref
  51.0 1.1 %lower.1 = (bf16[256,256]{1,0:T(8,128)(2,1)}, bf16[256,128]{1,0:T(8,128)(2,1)}) custom-call(bf16[256,512]{1,0:T(8,128)(2,1)S(1)} %get-tuple-element.23.t1_ref, f32[256,128]{1,0:T(8,128)S(1)} %get-tuple-element.27.kept_ref, bf16[256,384]{1,0:T(8,128)(2,1)S(1)} %collective-permute-done.1.near_ref, bf16[256,128]{1,0:T(8,128)(2,1)S(1)} %collective-permute-done.2.far_ref, ...), custom_call_target="tpu_custom_call" | custom-call | flops 1 | bytes 1 | tf_op jit(solution)/shard_map/lower/pallas_call | solution.py:272
  52.1 6.3 %all-to-all-done.2.r_ref = bf16[16,8,128]{2,1,0:T(8,128)(2,1)S(1)} async-done(((bf16[16,8,128]{2,1,0:T(8,128)(2,1)}), bf16[16,8,128]{2,1,0:T(8,128)(2,1)S(1)}, u32[]{:S(2)}, u32[]{:S(2)}) %all-to-all-start.2) | async-done | bytes 32800 | tf_op jit(solution)/shard_map/all_to_all | solution.py:318
  58.3 0.7 %final.1 = f32[16,64]{1,0:T(8,128)} custom-call(bf16[16,8,128]{2,1,0:T(8,128)(2,1)S(1)} %all-to-all-done.2.r_ref, bf16[256,128]{1,0:T(8,128)(2,1)} %get-tuple-element.38.after_ref), custom_call_target="tpu_custom_call" | custom-call | flops 20000 | bytes 40000 | tf_op jit(solution)/shard_map/final/pallas_call | solution.py:290
Async XLA Ops:
  0.6 0.9 %copy-start.1 = (bf16[64,1,3,256]{3,0,2,1:T(8,128)(2,1)S(1)}, bf16[64,1,3,256]{3,0,2,1:T(8,128)(2,1)}, u32[]{:S(2)}) copy-start(bf16[64,1,3,256]{3,0,2,1:T(8,128)(2,1)} %param.14) | copy-start | bytes 294916
  2.3 14.2 %all-to-all-start = ((bf16[4,3,64,256]{3,2,1,0:T(8,128)(2,1)}), bf16[4,3,64,256]{3,2,1,0:T(8,128)(2,1)S(1)}, u32[]{:S(2)}, u32[]{:S(2)}) async-start(bf16[4,3,64,256]{3,2,1,0:T(8,128)(2,1)} %spread.1), calls=%async_computation | async-start | bytes 786432 | tf_op jit(solution)/shard_map/all_to_all | solution.py:310
  7.2 7.9 %collective-permute-start = (bf16[128,4,256]{2,1,0:T(4,128)(2,1)}, bf16[128,4,256]{2,1,0:T(4,128)(2,1)S(1)}, u32[]{:S(2)}, u32[]{:S(2)}) collective-permute-start(bf16[128,4,256]{2,1,0:T(4,128)(2,1)} %bitcast.15), channel_id=1, source_target_pairs={{0,16},{16,0},{32,48},{48,32},{64,80},{80,64},{96,112},{112,96},{1... | collective-permute-start | bytes 786440 | tf_op jit(solution)/shard_map/ppermute | solution.py:301
  10.6 4.5 %copy-start = (bf16[128,1,4,256]{3,2,1,0:T(4,128)(2,1)S(1)}, bf16[128,1,4,256]{3,2,1,0:T(4,128)(2,1)}, u32[]{:S(2)}) copy-start(bf16[128,1,4,256]{3,2,1,0:T(4,128)(2,1)} %param.13) | copy-start | bytes 786436
  18.0 17.7 %all-to-all-start.1 = ((bf16[8,384,128]{2,1,0:T(8,128)(2,1)}), bf16[8,384,128]{2,1,0:T(8,128)(2,1)S(1)}, u32[]{:S(2)}, u32[]{:S(2)}) async-start(bf16[8,384,128]{2,1,0:T(8,128)(2,1)} %get-tuple-element.39), calls=%async_computation.1 | async-start | bytes 1572864 | tf_op jit(solution)/shard_map/all_to_all | solution.py:316
  26.1 24.9 %collective-permute-start.1 = (bf16[256,384]{1,0:T(8,128)(2,1)S(1)}, bf16[256,384]{1,0:T(8,128)(2,1)S(1)}, u32[]{:S(2)}, u32[]{:S(2)}) collective-permute-start(bf16[256,384]{1,0:T(8,128)(2,1)S(1)} %get-tuple-element.28), channel_id=1, source_target_pairs={{0,16},{16,0},{32,48},{48,32},{64,80},{80,64},{96,112},{112,96},{1... | collective-permute-start | bytes 589832 | tf_op jit(solution)/shard_map/ppermute | solution.py:301
  29.5 21.5 %collective-permute-start.2 = (bf16[256,128]{1,0:T(8,128)(2,1)S(1)}, bf16[256,128]{1,0:T(8,128)(2,1)S(1)}, u32[]{:S(2)}, u32[]{:S(2)}) collective-permute-start(bf16[256,128]{1,0:T(8,128)(2,1)S(1)} %get-tuple-element.29), channel_id=1, source_target_pairs={{0,32},{16,48},{32,0},{48,16},{64,96},{80,112},{96,64},{112,80},{1... | collective-permute-start | bytes 196616 | tf_op jit(solution)/shard_map/ppermute | solution.py:301
  33.8 17.2 %collective-permute-start.3 = (bf16[256,128]{1,0:T(8,128)(2,1)S(1)}, bf16[256,128]{1,0:T(8,128)(2,1)S(1)}, u32[]{:S(2)}, u32[]{:S(2)}) collective-permute-start(bf16[256,128]{1,0:T(8,128)(2,1)S(1)} %get-tuple-element.30), channel_id=1, source_target_pairs={{0,48},{16,32},{32,16},{48,0},{64,112},{80,96},{96,80},{112,64},{1... | collective-permute-start | bytes 196616 | tf_op jit(solution)/shard_map/ppermute | solution.py:301
  37.0 21.4 %all-to-all-start.2 = ((bf16[16,8,128]{2,1,0:T(8,128)(2,1)}), bf16[16,8,128]{2,1,0:T(8,128)(2,1)S(1)}, u32[]{:S(2)}, u32[]{:S(2)}) async-start(bf16[16,8,128]{2,1,0:T(8,128)(2,1)} %get-tuple-element.41), calls=%async_computation.2 | async-start | bytes 65536 | tf_op jit(solution)/shard_map/all_to_all | solution.py:318
